TPU v7x, 256 devices: a whole 4x4x8 slice. The times are simulated.
256 devices in a mesh: tile: 8 (over y, core), plane: 32 (over x, z).
Axes of the slice: x: 4, y: 4, z: 8, core: 2. Of those that a mesh axis runs over, the one named last changes fastest.
Arguments:
- observed: float32 [2, 32, 512, 256], P(None, 'plane', 'tile'), may hold values from 0.5 to 4
- intersection_strip: float32 [2, 32, 256, 256], P(None, 'plane', 'tile'), may hold values from 0.5 to 4
- axial_taps: float32 [2, 41], replicated, may hold values from 0.05 to 1
- lateral_taps: float32 [2, 15], replicated, may hold values from 0.05 to 1
- extents: int32 [8], P('tile'), may hold values from 1 to 32, as said below
- section_skews: int32 [8], P('tile'), may hold values from 0 to 255
Outputs:
- estimate: float32 [2, 32, 512, 256], P(None, 'plane', 'tile')
Inputs may be any that keep to these rules, and one draw needn't show every extreme that they name: `extents`: entry 0 is not used; the largest of the entries 1 to 7 is 32.
All inputs are finite; a program needn't handle non-finite values.
Results may differ from a plain program's by a relative error of at most 0.00005.
Values sent between devices are 32-bit elements; how exact they have to be, the bound alone decides.
A program may use at most 64 MiB of HBM per device.

v0:
```python
import jax
import jax.numpy as jnp
from jax import lax
from jax.sharding import PartitionSpec as P

ITERS = 2


highest = lax.Precision.HIGHEST


def with_halo(block, sides, width):
    for axis, dim in sides:
        count = lax.axis_size(axis)
        forward = [(i, i + 1) for i in range(count - 1)]
        backward = [(target, source) for source, target in forward]
        low = lax.ppermute(
            lax.slice_in_dim(block, block.shape[dim] - width, None, axis=dim), axis, forward
        )
        high = lax.ppermute(lax.slice_in_dim(block, 0, width, axis=dim), axis, backward)
        block = jnp.concatenate([low, block, high], axis=dim)
    return block


def from_behind(array, axis, by):
    length = lax.axis_size(axis)
    pairs = [(i, i + by) for i in range(length) if 0 <= i + by < length]
    return lax.ppermute(array, axis, pairs)


def band_matrix(kernel, row_count, col_count, offset):
    offsets = (
        jnp.arange(col_count, dtype=jnp.int32)[None, :]
        - jnp.arange(row_count, dtype=jnp.int32)[:, None]
        + offset
    )
    tap_ids = jnp.arange(kernel.shape[1], dtype=jnp.int32)
    one_hot = jnp.where(offsets[:, :, None] == tap_ids[None, None, :], 1.0, 0.0).astype(jnp.float32)
    return jnp.einsum("ck,rsk->crs", kernel, one_hot, precision=highest)


def blur_rows_x(volume, x_band):
    chans, planes, rowsn, voxels = volume.shape
    blocks = volume.reshape(chans, planes, rowsn, voxels // 128, 128)
    padded = jnp.pad(blocks, ((0, 0), (0, 0), (0, 0), (1, 1), (0, 0)))
    window = jnp.concatenate(
        [padded[:, :, :, :-2], padded[:, :, :, 1:-1], padded[:, :, :, 2:]], axis=4
    )
    result = jnp.einsum("czynw,cow->czyno", window, x_band, precision=highest)
    return result.reshape(chans, planes, rowsn, voxels)


def blur_rows_y(volume, y_band, half_width):
    padded = with_halo(volume, (("tile", 2),), half_width)
    return jnp.einsum("cyp,czpx->czyx", y_band, padded, precision=highest)


def axial_pass(pencils, z_band):
    return jnp.einsum("cij,cjw->ciw", z_band, pencils, precision=highest)


def to_pencils(volume):
    chans, planes, rowsn, voxels = volume.shape
    return lax.all_to_all(
        volume.reshape(chans, planes, rowsn * voxels),
        "plane",
        split_axis=2,
        concat_axis=1,
        tiled=True,
    )


def to_planes(pencils, row_count, col_count):
    flattened = lax.all_to_all(pencils, "plane", split_axis=1, concat_axis=2, tiled=True)
    return flattened.reshape(flattened.shape[0], flattened.shape[1], row_count, col_count)


def shards(observed, intersection_strip, axial_taps, lateral_taps, extents, section_skews):
    chans, planes, row_count, col_count = observed.shape
    strip_count = intersection_strip.shape[2]
    received = from_behind(intersection_strip, "tile", 1)
    turned = jnp.roll(received, section_skews[0], axis=3)
    reach_rows = jnp.where(lax.axis_index("tile") == 0, 0, extents[0])
    inside = (jnp.arange(strip_count, dtype=jnp.int32) < reach_rows)[None, None, :, None]
    top_rows = observed[:, :, :strip_count]
    joined_obs = jnp.concatenate(
        [jnp.where(inside, 0.5 * (top_rows + turned), top_rows), observed[:, :, strip_count:]],
        axis=2,
    )
    axial_width = axial_taps.shape[1]
    lateral_width = lateral_taps.shape[1]
    axial_half = axial_width // 2
    lateral_half = lateral_width // 2
    total_planes = planes * lax.axis_size("plane")
    axial_flip = jnp.flip(axial_taps, axis=1)
    lateral_flip = jnp.flip(lateral_taps, axis=1)
    z_forward = band_matrix(axial_taps, total_planes, total_planes, axial_half)
    z_adjoint = band_matrix(axial_flip, total_planes, total_planes, axial_half)
    y_forward = band_matrix(lateral_taps, row_count, row_count + 2 * lateral_half, 0)
    y_adjoint = band_matrix(lateral_flip, row_count, row_count + 2 * lateral_half, 0)
    x_forward = band_matrix(lateral_taps, 128, 384, lateral_half - 128)
    x_adjoint = band_matrix(lateral_flip, 128, 384, lateral_half - 128)
    estimate = joined_obs
    for sweep in range(ITERS):
        lateral_done = blur_rows_y(blur_rows_x(estimate, x_forward), y_forward, lateral_half)
        blurred = to_planes(axial_pass(to_pencils(lateral_done), z_forward), row_count, col_count)
        quotient = joined_obs / blurred
        spread_back = to_planes(axial_pass(to_pencils(quotient), z_adjoint), row_count, col_count)
        estimate = estimate * blur_rows_x(
            blur_rows_y(spread_back, y_adjoint, lateral_half), x_adjoint
        )
    return estimate


def solution(mesh):
    in_specs = (
        P(None, "plane", "tile", None),
        P(None, "plane", "tile", None),
        P(),
        P(),
        P("tile"),
        P("tile"),
    )
    out_specs = P(None, "plane", "tile", None)
    return jax.shard_map(shards, mesh=mesh, in_specs=in_specs, out_specs=out_specs, check_vma=False)
```

profile of v0, /device:TPU:1, one launch (start us, length us, event | category | flops | bytes accessed | tf_op | source)
XLA Modules:
  0.0 619.2 jit_solution(13503194051513561913)
XLA Ops:
  0.0 4.6 collective-permute-start
  6.0 3.3 fusion.10
  9.3 1.0 fusion.76
  10.5 0.6 fusion.20
  11.3 1.9 collective-permute-start.1
  13.3 2.4 collective-permute-start.2
  15.7 1.2 convolution_bitcast_fusion.5
  16.9 1.5 collective-permute-done.2
  18.6 4.6 copy.141
  23.2 0.5 broadcast.47
  23.8 74.4 %reduce = f32[16384,2]{1,0:T(8,128)} reduce(f32[16384,1,2]{2,1,0:T(1,128)} %bitcast.131, f32[]{:T(128)} %broadcast.47), dimensions={1}, to_apply=%bitcast.113.reduce_sub_computation | reduce | bytes 262148
  98.2 8.2 %reshape.294 = f32[32,1,1024]{2,1,0:T(1,128)} reshape(f32[16384,2]{1,0:T(8,128)} %reduce) | data formatting | bytes 262144
  106.4 11.2 %all-to-all-start = ((f32[32,1,1024]{2,1,0:T(1,128)}), f32[32,1,1024]{2,1,0:T(1,128)S(1)}, u32[]{:S(2)}, u32[]{:S(2)}) async-start(f32[32,1,1024]{2,1,0:T(1,128)} %reshape.294), calls=%async_computation | async-start | bytes 262144 | tf_op jit(solution)/shard_map/all_to_all | solution.py:64
  117.7 2.2 convolution_bitcast_fusion.6
  119.9 7.5 %all-to-all-done = f32[32,1,1024]{2,1,0:T(1,128)S(1)} async-done(((f32[32,1,1024]{2,1,0:T(1,128)}), f32[32,1,1024]{2,1,0:T(1,128)S(1)}, u32[]{:S(2)}, u32[]{:S(2)}) %all-to-all-start) | async-done | bytes 131104 | tf_op jit(solution)/shard_map/all_to_all | solution.py:64
  127.4 0.9 reduce.1
  128.3 14.9 %reshape.295 = f32[16384,1,2]{2,1,0:T(1,128)} reshape(f32[32,1024]{1,0:T(8,128)S(1)} %reduce.1) | data formatting | bytes 262144
  143.2 5.2 copy.142
  148.7 0.8 copy.104
  149.5 3.9 all-to-all-start.1
  153.5 9.1 %all-to-all-done.1 = f32[2,32,512]{2,0,1:T(2,128)S(1)} async-done(((f32[2,32,512]{2,0,1:T(2,128)}), f32[2,32,512]{2,0,1:T(2,128)S(1)}, u32[]{:S(2)}, u32[]{:S(2)}) %all-to-all-start.1) | async-done | bytes 131104 | tf_op jit(solution)/shard_map/all_to_all | solution.py:74
  162.6 12.1 %copy.105 = f32[2,1,16384]{0,1,2:T(1,128)} copy(f32[2,1,16384]{2,0,1:T(2,128)S(1)} %div.24) | data formatting | bytes 262144 | tf_op jit(solution)/shard_map/div | solution.py:107
  174.7 74.4 %reduce.2 = f32[16384,2]{1,0:T(8,128)} reduce(f32[16384,1,2]{2,1,0:T(1,128)} %bitcast.132, f32[]{:T(128)} %broadcast.47), dimensions={1}, to_apply=%bitcast.115.reduce_sub_computation | reduce | bytes 262148
  249.1 8.2 %reshape.296 = f32[32,1,1024]{2,1,0:T(1,128)} reshape(f32[16384,2]{1,0:T(8,128)} %reduce.2) | data formatting | bytes 262144
  257.4 4.8 all-to-all-start.2
  262.2 2.2 convolution_bitcast_fusion.7
  264.4 6.9 %all-to-all-done.2 = f32[32,1,1024]{2,1,0:T(1,128)S(1)} async-done(((f32[32,1,1024]{2,1,0:T(1,128)}), f32[32,1,1024]{2,1,0:T(1,128)S(1)}, u32[]{:S(2)}, u32[]{:S(2)}) %all-to-all-start.2) | async-done | bytes 131104 | tf_op jit(solution)/shard_map/all_to_all | solution.py:64
  271.3 0.9 reduce.3
  272.2 14.9 %reshape.297 = f32[16384,1,2]{2,1,0:T(1,128)} reshape(f32[32,1024]{1,0:T(8,128)S(1)} %reduce.3) | data formatting | bytes 262144
  287.1 5.2 copy.143
  292.6 0.8 copy.108
  293.4 3.9 all-to-all-start.3
  297.3 0.5 convolution_bitcast_fusion.4
  297.8 8.5 %all-to-all-done.3 = f32[2,32,512]{2,0,1:T(2,128)S(1)} async-done(((f32[2,32,512]{2,0,1:T(2,128)}), f32[2,32,512]{2,0,1:T(2,128)S(1)}, u32[]{:S(2)}, u32[]{:S(2)}) %all-to-all-start.3) | async-done | bytes 131104 | tf_op jit(solution)/shard_map/all_to_all | solution.py:74
  306.4 7.2 %collective-permute-start.3 = (f32[2,1,7,256]{3,2,0,1:T(8,128)S(1)}, f32[2,1,7,256]{3,2,0,1:T(8,128)S(1)}, u32[]{:S(2)}, u32[]{:S(2)}) collective-permute-start(f32[2,1,7,256]{3,2,0,1:T(8,128)S(1)} %get-tuple-element.15), channel_id=1, source_target_pairs={{0,32},{32,64},{64,96},{96,128},{128,160},{160,192},{192,224},{1,3... | collective-permute-start | bytes 43016 | tf_op jit(solution)/shard_map/ppermute | solution.py:17
  313.6 1.9 collective-permute-start.4
  315.5 2.6 fusion.13
  318.3 0.4 collective-permute-done.4
  319.0 0.6 fusion.25
  319.7 0.6 fusion.30
  320.6 3.3 collective-permute-start.5
  323.9 2.3 collective-permute-start.6
  326.2 2.7 collective-permute-done.6
  329.2 4.6 copy.148
  333.9 74.4 %reduce.4 = f32[16384,2]{1,0:T(8,128)} reduce(f32[16384,1,2]{2,1,0:T(1,128)} %bitcast.133, f32[]{:T(128)} %broadcast.47), dimensions={1}, to_apply=%bitcast.117.reduce_sub_computation | reduce | bytes 262148
  408.3 7.6 %reshape.298 = f32[32,1,1024]{2,1,0:T(1,128)S(1)} reshape(f32[16384,2]{1,0:T(8,128)} %reduce.4) | data formatting | bytes 262144
  415.9 12.5 %all_to_all.84 = f32[32,1,1024]{2,1,0:T(1,128)S(1)} all-to-all(f32[32,1,1024]{2,1,0:T(1,128)S(1)} %reshape.298), channel_id=1, replica_groups=mesh['tile'=8,'plane'=32] {'plane'}, dimensions={0} | all-to-all | bytes 262144 | tf_op jit(solution)/shard_map/all_to_all | solution.py:64
  428.4 0.9 reduce.5
  429.3 14.9 %reshape.299 = f32[16384,1,2]{2,1,0:T(1,128)} reshape(f32[32,1024]{1,0:T(8,128)S(1)} %reduce.5) | data formatting | bytes 262144
  444.2 5.2 copy.149
  449.8 12.7 %all_to_all.85 = f32[2,32,512]{2,0,1:T(2,128)S(1)} all-to-all(f32[2,32,512]{2,0,1:T(2,128)S(1)} %copy.123), channel_id=1, replica_groups=mesh['tile'=8,'plane'=32] {'plane'}, dimensions={1} | all-to-all | bytes 262144 | tf_op jit(solution)/shard_map/all_to_all | solution.py:74
  462.5 12.1 %copy.124 = f32[2,1,16384]{0,1,2:T(1,128)} copy(f32[2,1,16384]{2,0,1:T(2,128)S(1)} %div.25) | data formatting | bytes 262144 | tf_op jit(solution)/shard_map/div | solution.py:107
  474.7 74.4 %reduce.6 = f32[16384,2]{1,0:T(8,128)} reduce(f32[16384,1,2]{2,1,0:T(1,128)} %bitcast.134, f32[]{:T(128)} %broadcast.47), dimensions={1}, to_apply=%bitcast.119.reduce_sub_computation | reduce | bytes 262148
  549.1 7.6 %reshape.300 = f32[32,1,1024]{2,1,0:T(1,128)S(1)} reshape(f32[16384,2]{1,0:T(8,128)} %reduce.6) | data formatting | bytes 262144
  556.7 13.6 %all_to_all.86 = f32[32,1,1024]{2,1,0:T(1,128)S(1)} all-to-all(f32[32,1,1024]{2,1,0:T(1,128)S(1)} %reshape.300), channel_id=1, replica_groups=mesh['tile'=8,'plane'=32] {'plane'}, dimensions={0} | all-to-all | bytes 262144 | tf_op jit(solution)/shard_map/all_to_all | solution.py:64
  570.3 0.9 reduce.7
  571.2 14.9 %reshape.301 = f32[16384,1,2]{2,1,0:T(1,128)} reshape(f32[32,1024]{1,0:T(8,128)S(1)} %reduce.7) | data formatting | bytes 262144
  586.1 5.2 copy.150
  591.7 12.7 %all_to_all.87 = f32[2,32,512]{2,0,1:T(2,128)S(1)} all-to-all(f32[2,32,512]{2,0,1:T(2,128)S(1)} %copy.127), channel_id=1, replica_groups=mesh['tile'=8,'plane'=32] {'plane'}, dimensions={1} | all-to-all | bytes 262144 | tf_op jit(solution)/shard_map/all_to_all | solution.py:74
  604.5 7.6 %collective-permute-start.7 = (f32[2,1,7,256]{3,2,0,1:T(8,128)S(1)}, f32[2,1,7,256]{3,2,0,1:T(8,128)S(1)}, u32[]{:S(2)}, u32[]{:S(2)}) collective-permute-start(f32[2,1,7,256]{3,2,0,1:T(8,128)S(1)} %get-tuple-element.7), channel_id=1, source_target_pairs={{0,32},{32,64},{64,96},{96,128},{128,160},{160,192},{192,224},{1,3... | collective-permute-start | bytes 43016 | tf_op jit(solution)/shard_map/ppermute | solution.py:17
  612.1 1.9 collective-permute-start.8
  614.2 2.9 collective-permute-done.8
  617.5 0.6 fusion.35
  618.3 0.7 multiply_bitcast_fusion
  (58 shorter events, 4.2 us)
Async XLA Ops:
  0.0 9.3 %collective-permute-start = (f32[2,1,32,256]{3,2,0,1:T(8,128)}, f32[2,1,32,256]{3,2,0,1:T(8,128)S(1)}, u32[]{:S(2)}, u32[]{:S(2)}) collective-permute-start(f32[2,1,32,256]{3,2,0,1:T(8,128)} %bitcast.146), channel_id=1, source_target_pairs={{0,32},{32,64},{64,96},{96,128},{128,160},{160,192},{192,224},{1,3... | collective-permute-start | bytes 196616 | tf_op jit(solution)/shard_map/ppermute | solution.py:28
  11.3 5.5 collective-permute-start.1
  13.3 5.1 collective-permute-start.2
  98.2 19.5 %copy-start = (f32[2,41]{1,0:T(2,128)S(1)}, f32[2,41]{1,0:T(2,128)}, u32[]{:S(2)}) copy-start(f32[2,41]{1,0:T(2,128)} %param.8) | copy-start | bytes 988
  106.4 21.0 %all-to-all-start = ((f32[32,1,1024]{2,1,0:T(1,128)}), f32[32,1,1024]{2,1,0:T(1,128)S(1)}, u32[]{:S(2)}, u32[]{:S(2)}) async-start(f32[32,1,1024]{2,1,0:T(1,128)} %reshape.294), calls=%async_computation | async-start | bytes 262144 | tf_op jit(solution)/shard_map/all_to_all | solution.py:64
  149.5 13.0 %all-to-all-start.1 = ((f32[2,32,512]{2,0,1:T(2,128)}), f32[2,32,512]{2,0,1:T(2,128)S(1)}, u32[]{:S(2)}, u32[]{:S(2)}) async-start(f32[2,32,512]{2,0,1:T(2,128)} %copy.104), calls=%async_computation.1 | async-start | bytes 262144 | tf_op jit(solution)/shard_map/all_to_all | solution.py:74
  257.4 13.9 %all-to-all-start.2 = ((f32[32,1,1024]{2,1,0:T(1,128)}), f32[32,1,1024]{2,1,0:T(1,128)S(1)}, u32[]{:S(2)}, u32[]{:S(2)}) async-start(f32[32,1,1024]{2,1,0:T(1,128)} %reshape.296), calls=%async_computation.2 | async-start | bytes 262144 | tf_op jit(solution)/shard_map/all_to_all | solution.py:64
  272.2 25.0 %copy-start.1 = (f32[2,15]{1,0:T(2,128)S(1)}, f32[2,15]{1,0:T(2,128)}, u32[]{:S(2)}) copy-start(f32[2,15]{1,0:T(2,128)} %param.9) | copy-start | bytes 364
  293.4 13.0 %all-to-all-start.3 = ((f32[2,32,512]{2,0,1:T(2,128)}), f32[2,32,512]{2,0,1:T(2,128)S(1)}, u32[]{:S(2)}, u32[]{:S(2)}) async-start(f32[2,32,512]{2,0,1:T(2,128)} %copy.108), calls=%async_computation.3 | async-start | bytes 262144 | tf_op jit(solution)/shard_map/all_to_all | solution.py:74
  306.4 11.8 %collective-permute-start.3 = (f32[2,1,7,256]{3,2,0,1:T(8,128)S(1)}, f32[2,1,7,256]{3,2,0,1:T(8,128)S(1)}, u32[]{:S(2)}, u32[]{:S(2)}) collective-permute-start(f32[2,1,7,256]{3,2,0,1:T(8,128)S(1)} %get-tuple-element.15), channel_id=1, source_target_pairs={{0,32},{32,64},{64,96},{96,128},{128,160},{160,192},{192,224},{1,3... | collective-permute-start | bytes 43016 | tf_op jit(solution)/shard_map/ppermute | solution.py:17
  313.6 5.1 collective-permute-start.4
  320.6 5.6 collective-permute-start.5
  323.9 5.1 collective-permute-start.6
  604.5 9.8 %collective-permute-start.7 = (f32[2,1,7,256]{3,2,0,1:T(8,128)S(1)}, f32[2,1,7,256]{3,2,0,1:T(8,128)S(1)}, u32[]{:S(2)}, u32[]{:S(2)}) collective-permute-start(f32[2,1,7,256]{3,2,0,1:T(8,128)S(1)} %get-tuple-element.7), channel_id=1, source_target_pairs={{0,32},{32,64},{64,96},{96,128},{128,160},{160,192},{192,224},{1,3... | collective-permute-start | bytes 43016 | tf_op jit(solution)/shard_map/ppermute | solution.py:17
  612.1 5.1 collective-permute-start.8
where the time goes:
time: 628 us; the launch traced here: 619 us
  other arithmetic  303 us (48%)
  local copies, waits for them, and re-layouts  149 us (24%)
  starting transfers between devices  56.8 us (9%)
  blocking collectives  51.5 us (8%)
  waiting for transfers between devices  39.4 us (6%)
  matrix products  16.8 us (3%)
    unnamed x4, other arithmetic  298 us
    unnamed x13, local copies, waits for them, and re-layouts  91.8 us
    all_to_all x2, blocking collectives, to_pencils(): lax.all_to_all(volume.reshape(chans, planes, rowsn * voxels), 'plane', sp...  26.1 us
    all_to_all x2, blocking collectives, to_planes(): lax.all_to_all(pencils, 'plane', split_axis=1, concat_axis=2, tiled=True)  25.4 us
    div x2, local copies, waits for them, and re-layouts, shards(): quotient = joined_obs / blurred  24.2 us
    all_to_all x4, local copies, waits for them, and re-layouts, to_pencils(): lax.all_to_all(volume.reshape(chans, planes, rowsn * voxels), 'plane', sp...  20.8 us
    ppermute x4, starting transfers between devices, with_halo(): lax.ppermute(lax.slice_in_dim(block, block.shape[dim] - width, None, axis...  20 us
    all_to_all x2, waiting for transfers between devices, to_planes(): lax.all_to_all(pencils, 'plane', split_axis=1, concat_axis=2, tiled=True)  17.6 us
  transfers between devices with their start and end apart: 13, of which 8 were waited for; matrix products, arithmetic and copies ran while one was open for 2% of the time, Pallas kernels for 0%

commit v1 on v0

v1 whole, which is shorter than its diff:
```python
import functools

import jax
import jax.numpy as jnp
from jax import lax
from jax.experimental import pallas as pl
from jax.experimental.pallas import tpu as pltpu
from jax.sharding import PartitionSpec as P

F32 = jnp.float32
BF16 = jnp.bfloat16
MESH = pl.DeviceIdType.MESH
TILES, PLANES, ITERS = 8, 32, 2
KZ, KL = 41, 15


def pack_to_x(chan, half, tile):
    return 2 * ((chan + half * (tile % 2)) % 2) + half


def split(value):
    high = value.astype(BF16)
    return high, (value - high.astype(F32)).astype(BF16)


def lanes_of(shape):
    return lax.broadcasted_iota(jnp.int32, shape, len(shape) - 1)


def turn(value, by):
    by = by % 128
    return value if by == 0 else pltpu.roll(value, by, value.ndim - 1)


def build_lateral(taps, xt, out):
    lane = lanes_of((32, 128))
    row = lax.broadcasted_iota(jnp.int32, (32, 128), 0)
    x_out, y_out = lane % 32, lane // 32
    side, at = row // 8, row % 8
    own_diff = row - x_out + 7
    left = at - 8 - x_out + 7
    right = at + 32 - x_out + 7
    halo_diff = jnp.where((side == 0) & (xt > 0), left, -1)
    halo_diff = jnp.where((side == 3) & (xt < 7), right, halo_diff)
    blocks = []
    for diff in (own_diff, halo_diff):
        block = jnp.zeros((32, 128), F32)
        for j in range(KL):
            block = jnp.where(diff == j, taps[j], block)
        blocks.append(block)
    for d in range(5):
        for y_in in range(4):
            line = jnp.zeros((32, 128), F32)
            for y in range(4):
                k = 4 * (d - 2) + y_in - y + 7
                if 0 <= k < KL:
                    line = jnp.where(y_out == y, taps[k], line)
            for b, block in enumerate(blocks):
                high, low = split(block * line)
                rows = pl.ds(d * 256 + b * 128 + y_in * 32, 32)
                out[rows, 0:128] = high
                out[rows, 128:256] = low


def build_axial(taps, out):
    lane = lanes_of((32, 128))
    row = lax.broadcasted_iota(jnp.int32, (32, 128), 0)
    diff = lane % 32 - row + KZ // 2
    matrix = jnp.zeros((32, 128), F32)
    for j in range(KZ):
        matrix = jnp.where(diff == j, taps[j], matrix)
    high = matrix.astype(BF16).astype(F32)
    both = jnp.where(lane < 64, high, jnp.where(lane < 96, matrix - high, 0.0))
    out[...] = both.astype(BF16)


def kernel(
    observed, strip, axial, lateral, extents, skews, result,
    obs_v, strip_v, tx, rx, own, sl, sr, hl, hr, yh, ehi, elo, wf, wa, zf, za, ot, ox, res,
    obs_sem, strip_send, strip_recv, in_send, in_recv, halo_send, halo_recv, out_send, out_recv, res_sem,
):
    t = lax.axis_index("tile")
    p = lax.axis_index("plane")
    px, xt = p // 8, p % 8
    h = px % 2
    c = (px // 2 + h * (t % 2)) % 2
    slot = c * 16 + h * 8 + xt
    rr = 2 * t + h

    loads = []
    for ch in range(2):
        for half in range(2):
            loads.append(
                pltpu.make_async_copy(
                    observed.at[ch, 0, :, pl.ds(half * 128, 128)],
                    obs_v.at[pl.ds((ch * 2 + half) * 64, 64), :],
                    obs_sem.at[ch * 2 + half],
                )
            )
    for load in loads:
        load.start()

    def neighbour(dy, dx):
        there = (rr + dy + 2 * TILES) % (2 * TILES)
        tt, hh = there // 2, there % 2
        return {"tile": tt, "plane": pack_to_x(c, hh, tt) * 8 + (xt + dx + 8) % 8}

    barrier = pltpu.get_barrier_semaphore()

    def greet(i, _):
        pl.semaphore_signal(
            barrier, inc=1, device_id={"tile": t, "plane": (p + i) % PLANES}, device_id_type=MESH
        )
        return 0

    lax.fori_loop(1, PLANES, greet, 0)
    outward = jnp.where(h == 0, -1, 1)
    for dx in (-1, 0, 1):
        pl.semaphore_signal(barrier, inc=1, device_id=neighbour(outward, dx), device_id_type=MESH)
    after = {"tile": (t + 1) % TILES, "plane": p}
    before = {"tile": (t + TILES - 1) % TILES, "plane": p}
    for other in (after, before):
        pl.semaphore_signal(barrier, inc=1, device_id=other, device_id_type=MESH)
    pl.semaphore_wait(barrier, PLANES - 1 + 5)

    strips = []
    for ch in range(2):
        for half in range(2):
            strips.append(
                pltpu.make_async_remote_copy(
                    src_ref=strip.at[ch, 0, :, pl.ds(half * 128, 128)],
                    dst_ref=strip_v.at[pl.ds((ch * 2 + half) * 32, 32), :],
                    send_sem=strip_send.at[ch * 2 + half],
                    recv_sem=strip_recv.at[ch * 2 + half],
                    device_id=after,
                    device_id_type=MESH,
                )
            )
    for copy in strips:
        copy.start()
    for load in loads:
        load.wait()

    lane = lanes_of((8, 128))
    group = lane // 32

    def to_blocks(hh):
        for ch in range(2):
            for half in range(2):
                base = (ch * 2 + half) * 64 + hh * 32
                rows = [obs_v[pl.ds(base + y, 8, stride=4), :] for y in range(4)]
                for q in range(4):
                    tile = turn(rows[0], 32 * (0 - q))
                    for y in range(1, 4):
                        tile = jnp.where(group == y, turn(rows[y], 32 * (y - q)), tile)
                    tx[ch * 16 + hh * 8 + half * 4 + q] = tile

        def send(i, _):
            ch, xx = i // 8, (i + xt) % 8
            to = pack_to_x(ch, hh, t) * 8 + xx

            @pl.when(to != p)
            def _():
                pltpu.make_async_remote_copy(
                    src_ref=tx.at[ch * 16 + hh * 8 + xx],
                    dst_ref=rx.at[pl.ds(pl.multiple_of(p * 8, 8), 8), :],
                    send_sem=in_send,
                    recv_sem=in_recv,
                    device_id={"tile": t, "plane": to},
                    device_id_type=MESH,
                ).start()

            return 0

        lax.fori_loop(0, 16, send, 0)

    to_blocks(1)

    lat = [lateral[c, j] for j in range(KL)]
    ax = [axial[c, j] for j in range(KZ)]
    build_axial(ax, zf)
    build_lateral(lat, xt, wf)

    for copy in strips:
        copy.wait_recv()
    reach = jnp.where(t == 0, 0, extents[0])
    skew = skews[0]
    shift = skew % 128
    wide_lane = lanes_of((32, 128))
    inside = lax.broadcasted_iota(jnp.int32, (32, 128), 0) < reach
    for ch in range(2):
        low = strip_v[pl.ds(ch * 64, 32), :]
        high = strip_v[pl.ds(ch * 64 + 32, 32), :]
        low = pltpu.roll(low, shift, 1)
        high = pltpu.roll(high, shift, 1)
        wrapped = wide_lane < shift
        first = jnp.where(wrapped, high, low)
        second = jnp.where(wrapped, low, high)
        far = skew >= 128
        for half in range(2):
            moved = jnp.where(far, (second, first)[half], (first, second)[half])
            rows = pl.ds((ch * 2 + half) * 64, 32)
            top = obs_v[rows, :]
            obs_v[rows, :] = jnp.where(inside, 0.5 * (top + moved), top)
    to_blocks(0)
    rx[pl.ds(pl.multiple_of(p * 8, 8), 8), :] = tx[slot]

    build_axial(ax[::-1], za)
    build_lateral(lat[::-1], xt, wa)

    most = pl.ds(0, (PLANES - 1) * 8)
    pltpu.make_async_copy(rx.at[most, :], rx.at[most, :], in_recv).wait()
    joined = jnp.concatenate([rx[pl.ds(ys, 32, stride=8), :][None] for ys in range(8)], axis=0)

    edge = (lanes_of((8, 8, 128)) // 8) % 4
    edge12 = (lanes_of((12, 8, 128)) // 8) % 4
    row12 = lax.broadcasted_iota(jnp.int32, (12, 8, 128), 0)
    live12 = ((row12 >= 2) | (rr > 0)) & ((row12 < 10) | (rr < 2 * TILES - 1))

    def spread(value, w, z, n):
        own[n] = value
        parts = [value[:, 8 * k : 8 * k + 8, :] for k in range(4)]
        to_right = turn(parts[0], -24)
        to_left = parts[0]
        for k in range(1, 4):
            to_right = jnp.where(edge == k, turn(parts[k], 8 * k - 24), to_right)
            to_left = jnp.where(edge == k, turn(parts[k], 8 * k), to_left)
        sr[n] = to_right
        sl[n] = to_left
        copies = []
        for dx, source, target, sem in ((1, sr, hl, 0), (-1, sl, hr, 1)):
            for dy, rows, size, at in ((-1, 0, 2, 10), (0, 0, 8, 2), (1, 6, 2, 0)):
                copies.append((source.at[n, pl.ds(rows, size)], target.at[n, pl.ds(at, size)], sem, neighbour(dy, dx)))
        for dy, rows, at in ((-1, 0, 1), (1, 6, 0)):
            copies.append((own.at[n, pl.ds(rows, 2)], yh.at[n, at], 2, neighbour(dy, 0)))
        for source, target, sem, to in copies:
            pltpu.make_async_remote_copy(
                src_ref=source,
                dst_ref=target,
                send_sem=halo_send.at[n, sem],
                recv_sem=halo_recv.at[n, sem],
                device_id=to,
                device_id_type=MESH,
            ).start()
        ehi[2:10, :, 0:128], elo[2:10, :, 0:128] = split(value)
        pltpu.make_async_copy(yh.at[n], yh.at[n], halo_recv.at[n, 2]).wait()
        ehi[0:2, :, 0:128], elo[0:2, :, 0:128] = split(jnp.where(rr > 0, yh[n, 0], 0.0))
        ehi[10:12, :, 0:128], elo[10:12, :, 0:128] = split(jnp.where(rr < 2 * TILES - 1, yh[n, 1], 0.0))
        pltpu.make_async_copy(hl.at[n], hl.at[n], halo_recv.at[n, 0]).wait()
        pltpu.make_async_copy(hr.at[n], hr.at[n], halo_recv.at[n, 1]).wait()
        left = jnp.where(live12, hl[n], 0.0)
        right = jnp.where(live12, hr[n], 0.0)
        sides = [jnp.where(edge12 < 2, turn(left, -8 * k), turn(right, 24 - 8 * k)) for k in range(4)]
        ehi[:, :, 128:256], elo[:, :, 128:256] = split(jnp.concatenate(sides, axis=1))
        high = jnp.concatenate([ehi[d : d + 8].reshape(256, 256) for d in range(5)], axis=1)
        low = jnp.concatenate([elo[d : d + 8].reshape(256, 256) for d in range(5)], axis=1)
        both = jnp.dot(high, w[...], preferred_element_type=F32)
        flat = both[:, 0:128] + both[:, 128:256]
        flat = flat + jnp.dot(low, w[:, 0:128], preferred_element_type=F32)
        high, low = split(flat.reshape(8, 32, 128))
        stacked = jnp.concatenate([high, low, high], axis=1)
        wide = jnp.concatenate([stacked[ys] for ys in range(8)], axis=1)
        done = jnp.dot(z[:, 0:96], wide, preferred_element_type=F32)
        return jnp.concatenate([done[:, 128 * ys : 128 * ys + 128][None] for ys in range(8)], axis=0)

    estimate = joined
    for sweep in range(ITERS):
        blurred = spread(estimate, wf, zf, 2 * sweep)
        quotient = joined / blurred
        estimate = estimate * spread(quotient, wa, za, 2 * sweep + 1)

    for ys in range(8):
        ot[pl.ds(ys, 32, stride=8), :] = estimate[ys]

    def send_back(i, _):
        to = (p + i) % PLANES
        pltpu.make_async_remote_copy(
            src_ref=ot.at[pl.ds(pl.multiple_of(to * 8, 8), 8), :],
            dst_ref=ox.at[slot],
            send_sem=out_send,
            recv_sem=out_recv,
            device_id={"tile": t, "plane": to},
            device_id_type=MESH,
        ).start()
        return 0

    lax.fori_loop(1, PLANES, send_back, 0)
    ox[slot] = ot[pl.ds(pl.multiple_of(p * 8, 8), 8), :]
    few = pl.ds(0, PLANES - 1)
    pltpu.make_async_copy(ox.at[few], ox.at[few], out_recv).wait()
    stores = []
    for ch in range(2):
        for half in range(2):
            for hh in range(2):
                tiles = [ox[ch * 16 + hh * 8 + half * 4 + q] for q in range(4)]
                for y in range(4):
                    line = turn(tiles[0], 32 * (0 - y))
                    for q in range(1, 4):
                        line = jnp.where(group == q, turn(tiles[q], 32 * (q - y)), line)
                    res[pl.ds((ch * 2 + half) * 64 + hh * 32 + y, 8, stride=4), :] = line
            store = pltpu.make_async_copy(
                res.at[pl.ds((ch * 2 + half) * 64, 64), :],
                result.at[ch, 0, :, pl.ds(half * 128, 128)],
                res_sem.at[ch * 2 + half],
            )
            store.start()
            stores.append(store)

    for copy in strips:
        copy.wait_send()
    pltpu.make_async_copy(tx.at[few], tx.at[few], in_send).wait()
    for n in range(2 * ITERS):
        pltpu.make_async_copy(hl.at[n], hl.at[n], halo_send.at[n, 0]).wait()
        pltpu.make_async_copy(hr.at[n], hr.at[n], halo_send.at[n, 1]).wait()
        pltpu.make_async_copy(yh.at[n], yh.at[n], halo_send.at[n, 2]).wait()
    pltpu.make_async_copy(ox.at[few], ox.at[few], out_send).wait()
    for store in stores:
        store.wait()


def shards(observed, intersection_strip, axial_taps, lateral_taps, extents, section_skews):
    anywhere = pl.BlockSpec(memory_space=pl.ANY)
    scalars = pl.BlockSpec(memory_space=pltpu.SMEM)
    rounds = 2 * ITERS
    dma = pltpu.SemaphoreType.DMA
    return pl.pallas_call(
        kernel,
        out_shape=jax.ShapeDtypeStruct(observed.shape, F32),
        in_specs=[anywhere, anywhere, scalars, scalars, scalars, scalars],
        out_specs=anywhere,
        scratch_shapes=[
            pltpu.VMEM((256, 128), F32),
            pltpu.VMEM((128, 128), F32),
            pltpu.VMEM((32, 8, 128), F32),
            pltpu.VMEM((256, 128), F32),
            pltpu.VMEM((rounds, 8, 32, 128), F32),
            pltpu.VMEM((rounds, 8, 8, 128), F32),
            pltpu.VMEM((rounds, 8, 8, 128), F32),
            pltpu.VMEM((rounds, 12, 8, 128), F32),
            pltpu.VMEM((rounds, 12, 8, 128), F32),
            pltpu.VMEM((rounds, 2, 2, 32, 128), F32),
            pltpu.VMEM((12, 32, 256), BF16),
            pltpu.VMEM((12, 32, 256), BF16),
            pltpu.VMEM((1280, 256), BF16),
            pltpu.VMEM((1280, 256), BF16),
            pltpu.VMEM((32, 128), BF16),
            pltpu.VMEM((32, 128), BF16),
            pltpu.VMEM((256, 128), F32),
            pltpu.VMEM((32, 8, 128), F32),
            pltpu.VMEM((256, 128), F32),
            dma((4,)),
            dma((4,)),
            dma((4,)),
            dma,
            dma,
            dma((rounds, 3)),
            dma((rounds, 3)),
            dma,
            dma,
            dma((4,)),
        ],
        compiler_params=pltpu.CompilerParams(collective_id=0, has_side_effects=True),
        name="richardson_lucy",
    )(observed, intersection_strip, axial_taps, lateral_taps, extents, section_skews)


def solution(mesh):
    in_specs = (
        P(None, "plane", "tile", None),
        P(None, "plane", "tile", None),
        P(),
        P(),
        P("tile"),
        P("tile"),
    )
    out_specs = P(None, "plane", "tile", None)
    return jax.shard_map(shards, mesh=mesh, in_specs=in_specs, out_specs=out_specs, check_vma=False)
```

time: 628 us -> 53.7 us (0.09); the launches traced: 619 us -> 52.7 us
  other arithmetic: 303 us -> 0 us
  local copies, waits for them, and re-layouts: 149 us -> 1.57 us
  starting transfers between devices: 56.8 us -> 0 us
  blocking collectives: 51.5 us -> 0 us
  Pallas kernels: 0 us -> 49.8 us
  waiting for transfers between devices: 39.4 us -> 0 us
  matrix products: 16.8 us -> 0 us
    unnamed x4 -> x0, other arithmetic: 298 us -> none
    unnamed x13 -> x1, local copies, waits for them, and re-layouts: 91.8 us -> 1.57 us
    all_to_all x4 -> x0, blocking collectives: 51.5 us -> none  [the longest x2 26.1 us: to_pencils(): lax.all_to_all(volume.reshape(chans, planes, rowsn * voxels), 'plane', sp...]
    pallas_call x0 -> x1, Pallas kernels: none -> 49.8 us  [shards(): pl.pallas_call(kernel, out_shape=jax.ShapeDtypeStruct(observed.shape, F32...]
    ppermute x9 -> x0, starting transfers between devices: 33.1 us -> none  [the longest x4 20 us: with_halo(): lax.ppermute(lax.slice_in_dim(block, block.shape[dim] - width, None, axis...]
    all_to_all x4 -> x0, waiting for transfers between devices: 32 us -> none  [the longest x2 17.6 us: to_planes(): lax.all_to_all(pencils, 'plane', split_axis=1, concat_axis=2, tiled=True)]
    div x2 -> x0, local copies, waits for them, and re-layouts: 24.2 us -> none  [shards(): quotient = joined_obs / blurred]
    all_to_all x4 -> x0, starting transfers between devices: 23.7 us -> none  [the longest x2 16 us: to_pencils(): lax.all_to_all(volume.reshape(chans, planes, rowsn * voxels), 'plane', sp...]
  transfers between devices with their start and end apart: 13 -> 0, of which waited for: 8 -> 0; matrix products, arithmetic and copies ran while one was open for 2% -> 0% of each run, Pallas kernels for 0% -> 0%
where the time goes in v1:
time: 53.7 us; the launch traced here: 52.7 us
  Pallas kernels  49.8 us (93%)
  local copies, waits for them, and re-layouts  1.57 us (3%)
  between operations  1.3 us (2%)
    pallas_call x1, Pallas kernels, shards(): pl.pallas_call(kernel, out_shape=jax.ShapeDtypeStruct(observed.shape, F32...  49.8 us
    unnamed x1, local copies, waits for them, and re-layouts  1.57 us

profile of v1, /device:TPU:1, one launch (start us, length us, event | category | flops | bytes accessed | tf_op | source)
XLA Modules:
  0.0 52.7 jit_solution(9482365903629945683)
XLA Ops:
  1.3 49.8 %richardson_lucy.1 = f32[2,1,64,256]{3,2,1,0:T(8,128)} custom-call(f32[2,1,64,256]{3,2,1,0:T(8,128)} %observed.1, f32[2,1,32,256]{3,2,1,0:T(8,128)} %strip.1, f32[2,41]{1,0:T(2,128)} %axial.1, f32[2,15]{1,0:T(2,128)} %lateral.1, s32[1]{0:T(128)S(6)} %copy.8.extents, s32[1]{0:T(128)S(6)} %copy.9.skews), custom_call_target="tpu_custom_call" | custom-call | tf_op jit(solution)/shard_map/richardson_lucy/pallas_call | solution.py:326
  51.1 1.6 %copy.10 = f32[2,1,64,256]{3,2,1,0:T(8,128)} copy(f32[2,1,64,256]{3,2,1,0:T(8,128)} %richardson_lucy.1) | data formatting | bytes 262144

commit v2 on v1

v2 whole, which is shorter than its diff:
```python
import jax
import jax.numpy as jnp
from jax import lax
from jax.experimental import pallas as pl
from jax.experimental.pallas import tpu as pltpu
from jax.sharding import PartitionSpec as P

F32 = jnp.float32
BF16 = jnp.bfloat16
MESH = pl.DeviceIdType.MESH
TILES, PLANES, ITERS = 8, 32, 2
KZ, KL = 41, 15


def home_of(chan, row, xt):
    y, turn_x, q = row // 4, row % 4, xt // 2
    px = jnp.where(y % 2 == 0, turn_x, 3 - turn_x)
    return {"tile": 2 * y + (xt + q) % 2, "plane": 8 * px + 4 * chan + q}


def split(value):
    high = value.astype(BF16)
    return high, (value - high.astype(F32)).astype(BF16)


def lanes_of(shape):
    return lax.broadcasted_iota(jnp.int32, shape, len(shape) - 1)


def turn(value, by):
    by = by % 128
    return value if by == 0 else pltpu.roll(value, by, value.ndim - 1)


def build_lateral(taps, out):
    lane = lanes_of((32, 128))
    row = lax.broadcasted_iota(jnp.int32, (32, 128), 0)
    x_out, y_out = lane % 32, lane // 32
    side, at = row // 8, row % 8
    own_diff = row - x_out + 7
    left = at - 8 - x_out + 7
    right = at + 32 - x_out + 7
    halo_diff = jnp.where(side == 0, left, jnp.where(side == 3, right, -1))
    blocks = []
    for diff in (own_diff, halo_diff):
        block = jnp.zeros((32, 128), F32)
        for j in range(KL):
            block = jnp.where(diff == j, taps[j], block)
        blocks.append(block)
    for d in range(5):
        for y_in in range(4):
            line = jnp.zeros((32, 128), F32)
            for y in range(4):
                k = 4 * (d - 2) + y_in - y + 7
                if 0 <= k < KL:
                    line = jnp.where(y_out == y, taps[k], line)
            for b, block in enumerate(blocks):
                high, low = split(block * line)
                rows = pl.ds(b * 640 + d * 128 + y_in * 32, 32)
                out[rows, 0:128] = high
                out[rows, 128:256] = low


def build_axial(taps, out):
    lane = lanes_of((32, 128))
    row = lax.broadcasted_iota(jnp.int32, (32, 128), 0)
    diff = lane % 32 - row + KZ // 2
    matrix = jnp.zeros((32, 128), F32)
    for j in range(KZ):
        matrix = jnp.where(diff == j, taps[j], matrix)
    high = matrix.astype(BF16).astype(F32)
    both = jnp.where(lane < 64, high, jnp.where(lane < 96, matrix - high, 0.0))
    out[...] = both.astype(BF16)


def far_first(i):
    return 4 + ((i + 1) // 2) * (1 - 2 * (i % 2))


def kernel(
    observed, strip, axial, lateral, extents, skews, ox,
    obs_v, strip_s, strip_v, tx, rx, own, sl, sr, hl, hr, yh, eo, eh, wf, wa, zf, za, ot,
    obs_sem, strip_load, strip_send, strip_recv, in_send, in_recv, halo_send, halo_recv, out_send, out_recv,
):
    t = lax.axis_index("tile")
    p = lax.axis_index("plane")
    px, pz = p // 8, p % 8
    y, core = t // 2, t % 2
    c, q_own = pz // 4, pz % 4
    xt = 2 * q_own + (core + q_own) % 2
    rr = 4 * y + jnp.where(y % 2 == 0, px, 3 - px)
    h = rr % 2
    source = rr // 2
    slot = c * 16 + h * 8 + xt
    at_home = source == t

    loads = []
    strip_loads = []
    for ch in range(2):
        for half in range(2):
            i = ch * 2 + half
            lanes = pl.ds(half * 128, 128)
            strip_loads.append(
                pltpu.make_async_copy(strip.at[ch, 0, :, lanes], strip_s.at[pl.ds(i * 32, 32), :], strip_load.at[i])
            )
            loads.append(
                pltpu.make_async_copy(observed.at[ch, 0, :, lanes], obs_v.at[pl.ds(i * 64, 64), :], obs_sem.at[i])
            )
    for load in strip_loads + loads:
        load.start()

    strip_v[...] = jnp.zeros(strip_v.shape, F32)
    hl[...] = jnp.zeros(hl.shape, F32)
    hr[...] = jnp.zeros(hr.shape, F32)
    yh[...] = jnp.zeros(yh.shape, F32)

    def exists(dy, dx):
        fine = (xt + dx >= 0) & (xt + dx < 8)
        return fine & (rr + dy >= 0) & (rr + dy < 2 * TILES)

    around = [(dy, dx) for dy in (-1, 1) for dx in (-1, 1)] + [(0, -1), (0, 1), (-1, 0), (1, 0)]
    after = {"tile": t + 1, "plane": p}
    before = {"tile": t - 1, "plane": p}

    barrier = pltpu.get_barrier_semaphore()

    def greet(to):
        pl.semaphore_signal(barrier, inc=1, device_id=to, device_id_type=MESH)

    def greet_blocks(i, _):
        zz = (pz + far_first(i)) % 8
        for hh in range(2):
            for cc in range(2):
                to = home_of(zz // 4, 2 * t + hh, 2 * (zz % 4) + cc)

                @pl.when((to["plane"] != p) | (to["tile"] != t))
                def _():
                    greet(to)

        low = jnp.where((core + y) % 2 == 0, 2, 0)
        for xx in range(2):
            greet({"tile": source, "plane": 8 * (low + xx) + zz})
        return 0

    lax.fori_loop(0, 8, greet_blocks, 0)
    met = 48 - jnp.where(at_home, 1, 0)
    for dy, dx in around:

        @pl.when(exists(dy, dx))
        def _():
            greet(home_of(c, rr + dy, xt + dx))

        met = met + jnp.where(exists(dy, dx), 1, 0)

    @pl.when(t < TILES - 1)
    def _():
        greet(after)

    @pl.when(t > 0)
    def _():
        greet(before)

    met = met + jnp.where(t < TILES - 1, 1, 0) + jnp.where(t > 0, 1, 0)

    lane = lanes_of((8, 128))
    group = lane // 32

    def to_blocks(hh):
        for ch in range(2):
            for half in range(2):
                base = (ch * 2 + half) * 64 + hh * 32
                rows = [obs_v[pl.ds(base + y, 8, stride=4), :] for y in range(4)]
                for q in range(4):
                    tile = turn(rows[0], 32 * (0 - q))
                    for y in range(1, 4):
                        tile = jnp.where(group == y, turn(rows[y], 32 * (y - q)), tile)
                    tx[ch * 16 + hh * 8 + half * 4 + q] = tile

    def send_blocks(hh):
        def send(i, _):
            zz = (pz + far_first(i)) % 8
            for cc in range(2):
                xx = 2 * (zz % 4) + cc
                to = home_of(zz // 4, 2 * t + hh, xx)

                @pl.when((to["plane"] != p) | (to["tile"] != t))
                def _():
                    pltpu.make_async_remote_copy(
                        src_ref=tx.at[(zz // 4) * 16 + hh * 8 + xx],
                        dst_ref=rx.at[pl.ds(pl.multiple_of(p * 8, 8), 8), :],
                        send_sem=in_send,
                        recv_sem=in_recv,
                        device_id=to,
                        device_id_type=MESH,
                    ).start()

            return 0

        lax.fori_loop(0, 8, send, 0)

    for load in loads + strip_loads:
        load.wait()
    to_blocks(1)
    pl.semaphore_wait(barrier, met)

    strips = []
    for i in range(4):
        rows = pl.ds(i * 32, 32)
        strips.append(
            pltpu.make_async_remote_copy(
                src_ref=strip_s.at[rows, :],
                dst_ref=strip_v.at[rows, :],
                send_sem=strip_send.at[i],
                recv_sem=strip_recv.at[i],
                device_id=after,
                device_id_type=MESH,
            )
        )

    @pl.when(t < TILES - 1)
    def _():
        for copy in strips:
            copy.start()

    send_blocks(1)

    lat = [lateral[c, j] for j in range(KL)]
    ax = [axial[c, j] for j in range(KZ)]
    build_axial(ax, zf)
    build_lateral(lat, wf)
    eo[...] = jnp.zeros(eo.shape, BF16)
    eh[...] = jnp.zeros(eh.shape, BF16)

    @pl.when(t > 0)
    def _():
        for copy in strips:
            copy.wait_recv()

    reach = jnp.where(t == 0, 0, extents[0])
    skew = skews[0]
    shift = skew % 128
    wide_lane = lanes_of((32, 128))
    inside = lax.broadcasted_iota(jnp.int32, (32, 128), 0) < reach
    for ch in range(2):
        low = strip_v[pl.ds(ch * 64, 32), :]
        high = strip_v[pl.ds(ch * 64 + 32, 32), :]
        low = pltpu.roll(low, shift, 1)
        high = pltpu.roll(high, shift, 1)
        wrapped = wide_lane < shift
        first = jnp.where(wrapped, high, low)
        second = jnp.where(wrapped, low, high)
        far = skew >= 128
        for half in range(2):
            moved = jnp.where(far, (second, first)[half], (first, second)[half])
            rows = pl.ds((ch * 2 + half) * 64, 32)
            top = obs_v[rows, :]
            obs_v[rows, :] = jnp.where(inside, 0.5 * (top + moved), top)
    to_blocks(0)
    send_blocks(0)

    @pl.when(at_home)
    def _():
        rx[pl.ds(pl.multiple_of(p * 8, 8), 8), :] = tx[slot]

    build_axial(ax[::-1], za)
    build_lateral(lat[::-1], wa)

    @pl.when(at_home)
    def _():
        most = pl.ds(0, (PLANES - 1) * 8)
        pltpu.make_async_copy(rx.at[most, :], rx.at[most, :], in_recv).wait()

    @pl.when(jnp.logical_not(at_home))
    def _():
        pltpu.make_async_copy(rx, rx, in_recv).wait()

    joined = jnp.concatenate([rx[pl.ds(ys, 32, stride=8), :][None] for ys in range(8)], axis=0)

    edge = (lanes_of((8, 8, 128)) // 8) % 4
    edge2 = (lanes_of((2, 8, 128)) // 8) % 4
    sent = []

    def banded(high, low, w, first, last):
        both = jnp.dot(high, w[first:last, :], preferred_element_type=F32)
        more = jnp.dot(low, w[first:last, 0:128], preferred_element_type=F32)
        return both[:, 0:128] + both[:, 128:256] + more

    def along_z(flat, z):
        n = flat.shape[0] // 32
        high, low = split(flat.reshape(n, 32, 128))
        stacked = jnp.concatenate([high, low, high], axis=1)
        wide = jnp.concatenate([stacked[i] for i in range(n)], axis=1)
        done = jnp.dot(z[:, 0:96], wide, preferred_element_type=F32)
        return [done[:, 128 * i : 128 * i + 128] for i in range(n)]

    def shifted(pad, value, w, base):
        pad[0, 2:10], pad[1, 2:10] = split(value)
        wide = [jnp.concatenate([pad[s, d : d + 8].reshape(256, 128) for d in range(5)], axis=1) for s in range(2)]
        return banded(wide[0], wide[1], w, base, base + 640)

    def unpack(left, right, which):
        sides = [jnp.where(which < 2, turn(left, -8 * k), turn(right, 24 - 8 * k)) for k in range(4)]
        return jnp.concatenate(sides, axis=1)

    def spread(value, w, z, n):
        own[n] = value
        parts = [value[:, 8 * k : 8 * k + 8, :] for k in range(4)]
        to_right = turn(parts[0], -24)
        to_left = parts[0]
        for k in range(1, 4):
            to_right = jnp.where(edge == k, turn(parts[k], 8 * k - 24), to_right)
            to_left = jnp.where(edge == k, turn(parts[k], 8 * k), to_left)
        sr[n] = to_right
        sl[n] = to_left
        copies = {}
        for i, (dy, dx) in enumerate(around):
            rows, size, at = {-1: (0, 2, 10), 0: (0, 8, 2), 1: (6, 2, 0)}[dy]
            if dx == 0:
                src, dst = own.at[n, pl.ds(rows, 2)], yh.at[n, 0 if dy == 1 else 1]
            else:
                src = (sr if dx == 1 else sl).at[n, pl.ds(rows, size)]
                dst = (hl if dx == 1 else hr).at[n, pl.ds(at, size)]
            copy = pltpu.make_async_remote_copy(
                src_ref=src,
                dst_ref=dst,
                send_sem=halo_send.at[n, i],
                recv_sem=halo_recv.at[n, i],
                device_id=home_of(c, rr + dy, xt + dx),
                device_id_type=MESH,
            )
            copies[dy, dx] = copy

            @pl.when(exists(dy, dx))
            def _():
                copy.start()

            sent.append((exists(dy, dx), copy))

        def arrive(dy, dx):
            @pl.when(exists(-dy, -dx))
            def _():
                copies[dy, dx].wait_recv()

        whole = along_z(shifted(eo, value, w, 0), z)
        arrive(0, 1)
        arrive(0, -1)
        beside = unpack(hl[n, 2:10], hr[n, 2:10], edge)
        sides = along_z(shifted(eh, beside, w, 640), z)
        whole = [a + b for a, b in zip(whole, sides)]
        for dy, dx in around:
            if dy != 0:
                arrive(dy, dx)
        ends = []
        for at, rows in ((0, 0), (1, 10)):
            corner = unpack(hl[n, rows : rows + 2], hr[n, rows : rows + 2], edge2)
            ends.append([split(yh[n, at]), split(corner)])
        flat = []
        for at in range(2):
            total = None
            for b in range(2):
                wide = []
                for s in range(2):
                    pair = ends[at][b][s]
                    none = jnp.zeros((32, 128), BF16)
                    if at == 0:
                        lines = ((pair[0], pair[1]), (pair[1], none))
                    else:
                        lines = ((none, pair[0]), (pair[0], pair[1]))
                    wide.append(jnp.concatenate([jnp.concatenate(line, axis=1) for line in lines], axis=0))
                first = b * 640 + (0 if at == 0 else 3 * 128)
                part = banded(wide[0], wide[1], w, first, first + 256)
                total = part if total is None else total + part
            flat.append(total)
        outer = along_z(jnp.concatenate(flat, axis=0), z)
        for i, ys in enumerate((0, 1, 6, 7)):
            whole[ys] = whole[ys] + outer[i]
        return jnp.concatenate([line[None] for line in whole], axis=0)

    estimate = joined
    for sweep in range(ITERS):
        blurred = spread(estimate, wf, zf, 2 * sweep)
        quotient = joined / blurred
        estimate = estimate * spread(quotient, wa, za, 2 * sweep + 1)

    for ys in range(8):
        ot[pl.ds(ys, 32, stride=8), :] = estimate[ys]

    def send_back(i, _):
        zz = (pz + far_first(i)) % 8
        for dx in (2, 1, 3, 0):
            to = 8 * ((px + dx) % 4) + zz

            @pl.when((to != p) | jnp.logical_not(at_home))
            def _():
                pltpu.make_async_remote_copy(
                    src_ref=ot.at[pl.ds(pl.multiple_of(to * 8, 8), 8), :],
                    dst_ref=ox.at[slot],
                    send_sem=out_send,
                    recv_sem=out_recv,
                    device_id={"tile": source, "plane": to},
                    device_id_type=MESH,
                ).start()

        return 0

    lax.fori_loop(0, 8, send_back, 0)

    @pl.when(at_home)
    def _():
        ox[slot] = ot[pl.ds(pl.multiple_of(p * 8, 8), 8), :]

    @pl.when(t < TILES - 1)
    def _():
        for copy in strips:
            copy.wait_send()

    for there, copy in sent:

        @pl.when(there)
        def _():
            copy.wait_send()

    @pl.when(at_home)
    def _():
        few = pl.ds(0, PLANES - 1)
        pltpu.make_async_copy(tx.at[few], tx.at[few], in_send).wait()
        pltpu.make_async_copy(ox.at[few], ox.at[few], out_recv).wait()
        pltpu.make_async_copy(ox.at[few], ox.at[few], out_send).wait()

    @pl.when(jnp.logical_not(at_home))
    def _():
        pltpu.make_async_copy(tx, tx, in_send).wait()
        pltpu.make_async_copy(ox, ox, out_recv).wait()
        pltpu.make_async_copy(ox, ox, out_send).wait()


def to_rows(ox, result, res, sem):
    group = lanes_of((8, 128)) // 32
    stores = []
    for ch in range(2):
        for half in range(2):
            for hh in range(2):
                tiles = [ox[ch * 16 + hh * 8 + half * 4 + q] for q in range(4)]
                for y in range(4):
                    line = turn(tiles[0], 32 * (0 - y))
                    for q in range(1, 4):
                        line = jnp.where(group == q, turn(tiles[q], 32 * (q - y)), line)
                    res[pl.ds((ch * 2 + half) * 64 + hh * 32 + y, 8, stride=4), :] = line
            store = pltpu.make_async_copy(
                res.at[pl.ds((ch * 2 + half) * 64, 64), :],
                result.at[ch, 0, :, pl.ds(half * 128, 128)],
                sem.at[ch * 2 + half],
            )
            store.start()
            stores.append(store)
    for store in stores:
        store.wait()


def shards(observed, intersection_strip, axial_taps, lateral_taps, extents, section_skews):
    anywhere = pl.BlockSpec(memory_space=pl.ANY)
    scalars = pl.BlockSpec(memory_space=pltpu.SMEM)
    vmem = pl.BlockSpec(memory_space=pltpu.VMEM)
    rounds = 2 * ITERS
    dma = pltpu.SemaphoreType.DMA
    blocks = pl.pallas_call(
        kernel,
        out_shape=jax.ShapeDtypeStruct((32, 8, 128), F32),
        in_specs=[anywhere, anywhere, scalars, scalars, scalars, scalars],
        out_specs=vmem,
        scratch_shapes=[
            pltpu.VMEM((256, 128), F32),
            pltpu.VMEM((128, 128), F32),
            pltpu.VMEM((128, 128), F32),
            pltpu.VMEM((32, 8, 128), F32),
            pltpu.VMEM((256, 128), F32),
            pltpu.VMEM((rounds, 8, 32, 128), F32),
            pltpu.VMEM((rounds, 8, 8, 128), F32),
            pltpu.VMEM((rounds, 8, 8, 128), F32),
            pltpu.VMEM((rounds, 12, 8, 128), F32),
            pltpu.VMEM((rounds, 12, 8, 128), F32),
            pltpu.VMEM((rounds, 2, 2, 32, 128), F32),
            pltpu.VMEM((2, 12, 32, 128), BF16),
            pltpu.VMEM((2, 12, 32, 128), BF16),
            pltpu.VMEM((1280, 256), BF16),
            pltpu.VMEM((1280, 256), BF16),
            pltpu.VMEM((32, 128), BF16),
            pltpu.VMEM((32, 128), BF16),
            pltpu.VMEM((256, 128), F32),
            dma((4,)),
            dma((4,)),
            dma((4,)),
            dma((4,)),
            dma,
            dma,
            dma((rounds, 8)),
            dma((rounds, 8)),
            dma,
            dma,
        ],
        compiler_params=pltpu.CompilerParams(collective_id=0, has_side_effects=True),
        name="richardson_lucy",
    )(observed, intersection_strip, axial_taps, lateral_taps, extents, section_skews)
    return pl.pallas_call(
        to_rows,
        out_shape=jax.ShapeDtypeStruct(observed.shape, F32),
        in_specs=[vmem],
        out_specs=anywhere,
        scratch_shapes=[pltpu.VMEM((256, 128), F32), dma((4,))],
        name="rows_of_blocks",
    )(blocks)


def solution(mesh):
    in_specs = (
        P(None, "plane", "tile", None),
        P(None, "plane", "tile", None),
        P(),
        P(),
        P("tile"),
        P("tile"),
    )
    out_specs = P(None, "plane", "tile", None)
    return jax.shard_map(shards, mesh=mesh, in_specs=in_specs, out_specs=out_specs, check_vma=False)
```

time: 53.7 us -> 46.5 us (0.87); the launches traced: 52.7 us -> 46.3 us
  Pallas kernels: 49.8 us -> 45 us
  local copies, waits for them, and re-layouts: 1.57 us -> 0 us
    pallas_call x1 -> x2, Pallas kernels: 49.8 us -> 45 us  [the longest x1 43.3 us: shards(): pl.pallas_call(kernel, out_shape=jax.ShapeDtypeStruct((32, 8, 128), F32),...]
    unnamed x1 -> x0, local copies, waits for them, and re-layouts: 1.57 us -> none
where the time goes in v2:
time: 46.5 us; the launch traced here: 46.3 us
  Pallas kernels  45 us (97%)
  between operations  1.3 us (3%)
    pallas_call x1, Pallas kernels, shards(): pl.pallas_call(kernel, out_shape=jax.ShapeDtypeStruct((32, 8, 128), F32),...  43.3 us
    pallas_call x1, Pallas kernels, shards(): pl.pallas_call(to_rows, out_shape=jax.ShapeDtypeStruct(observed.shape, F3...  1.72 us

profile of v2, /device:TPU:1, one launch (start us, length us, event | category | flops | bytes accessed | tf_op | source)
XLA Modules:
  0.0 46.3 jit_solution(4954060500915009057)
XLA Ops:
  1.3 43.3 %richardson_lucy.1.ox = f32[32,8,128]{2,1,0:T(8,128)} custom-call(f32[2,1,64,256]{3,2,1,0:T(8,128)} %observed.1, f32[2,1,32,256]{3,2,1,0:T(8,128)} %strip.1, f32[2,41]{1,0:T(2,128)} %axial.1, f32[2,15]{1,0:T(2,128)} %lateral.1, s32[1]{0:T(128)S(6)} %copy.7.extents, s32[1]{0:T(128)S(6)} %copy.8.skews), custom_call_target="tpu_custom_call" | custom-call | tf_op jit(solution)/shard_map/richardson_lucy/pallas_call | solution.py:466
  44.6 1.7 %rows_of_blocks.1 = f32[2,1,64,256]{3,2,1,0:T(8,128)} custom-call(f32[32,8,128]{2,1,0:T(8,128)} %richardson_lucy.1.ox), custom_call_target="tpu_custom_call" | custom-call | tf_op jit(solution)/shard_map/rows_of_blocks/pallas_call | solution.py:504

commit v3 on v2

--- a/solution.py
+++ b/solution.py
@@ -13,9 +13,9 @@
 
 
 def home_of(chan, row, xt):
-    y, turn_x, q = row // 4, row % 4, xt // 2
-    px = jnp.where(y % 2 == 0, turn_x, 3 - turn_x)
-    return {"tile": 2 * y + (xt + q) % 2, "plane": 8 * px + 4 * chan + q}
+    y, turn_x, q = lax.div(row, 4), lax.rem(row, 4), lax.div(xt, 2)
+    px = turn_x + lax.rem(y, 2) * (3 - 2 * turn_x)
+    return {"tile": 2 * y + lax.rem(xt + q, 2), "plane": 8 * px + 4 * chan + q}
 
 
 def split(value):
@@ -73,8 +73,7 @@
     out[...] = both.astype(BF16)
 
 
-def far_first(i):
-    return 4 + ((i + 1) // 2) * (1 - 2 * (i % 2))
+FAR_FIRST = (4, 3, 5, 2, 6, 1, 7, 0)
 
 
 def kernel(
@@ -84,15 +83,54 @@
 ):
     t = lax.axis_index("tile")
     p = lax.axis_index("plane")
-    px, pz = p // 8, p % 8
-    y, core = t // 2, t % 2
-    c, q_own = pz // 4, pz % 4
-    xt = 2 * q_own + (core + q_own) % 2
-    rr = 4 * y + jnp.where(y % 2 == 0, px, 3 - px)
-    h = rr % 2
-    source = rr // 2
+    px, pz = lax.div(p, 8), lax.rem(p, 8)
+    y, core = lax.div(t, 2), lax.rem(t, 2)
+    c, q_own = lax.div(pz, 4), lax.rem(pz, 4)
+    xt = 2 * q_own + lax.rem(core + q_own, 2)
+    rr = 4 * y + px + lax.rem(y, 2) * (3 - 2 * px)
+    h = lax.rem(rr, 2)
+    source = lax.div(rr, 2)
     slot = c * 16 + h * 8 + xt
     at_home = source == t
+
+    def exists(dy, dx):
+        fine = (xt + dx >= 0) & (xt + dx < 8)
+        return fine & (rr + dy >= 0) & (rr + dy < 2 * TILES)
+
+    around = [(dy, dx) for dy in (-1, 1) for dx in (-1, 1)] + [(0, -1), (0, 1), (-1, 0), (1, 0)]
+    after = {"tile": t + 1, "plane": p}
+    before = {"tile": t - 1, "plane": p}
+
+    barrier = pltpu.get_barrier_semaphore()
+
+    def greet(to):
+        pl.semaphore_signal(barrier, inc=1, device_id=to, device_id_type=MESH)
+
+    for dz in FAR_FIRST:
+        for dx in (2, 1, 3, 0):
+            to = 8 * lax.rem(px + dx, 4) + lax.rem(pz + dz, 8)
+            if dz + dx == 0:
+
+                @pl.when(source != t)
+                def _():
+                    greet({"tile": source, "plane": to})
+
+            else:
+                greet({"tile": source, "plane": to})
+    met = PLANES - jnp.where(at_home, 1, 0)
+    for dy, dx in around:
+
+        @pl.when(exists(dy, dx))
+        def _():
+            greet(home_of(c, rr + dy, xt + dx))
+
+        met = met + jnp.where(exists(dy, dx), 1, 0)
+
+    @pl.when(t > 0)
+    def _():
+        greet(before)
+
+    met = met + jnp.where(t < TILES - 1, 1, 0)
 
     loads = []
     strip_loads = []
@@ -109,58 +147,28 @@
     for load in strip_loads + loads:
         load.start()
 
-    strip_v[...] = jnp.zeros(strip_v.shape, F32)
-    hl[...] = jnp.zeros(hl.shape, F32)
-    hr[...] = jnp.zeros(hr.shape, F32)
-    yh[...] = jnp.zeros(yh.shape, F32)
-
-    def exists(dy, dx):
-        fine = (xt + dx >= 0) & (xt + dx < 8)
-        return fine & (rr + dy >= 0) & (rr + dy < 2 * TILES)
-
-    around = [(dy, dx) for dy in (-1, 1) for dx in (-1, 1)] + [(0, -1), (0, 1), (-1, 0), (1, 0)]
-    after = {"tile": t + 1, "plane": p}
-    before = {"tile": t - 1, "plane": p}
-
-    barrier = pltpu.get_barrier_semaphore()
-
-    def greet(to):
-        pl.semaphore_signal(barrier, inc=1, device_id=to, device_id_type=MESH)
-
-    def greet_blocks(i, _):
-        zz = (pz + far_first(i)) % 8
-        for hh in range(2):
-            for cc in range(2):
-                to = home_of(zz // 4, 2 * t + hh, 2 * (zz % 4) + cc)
-
-                @pl.when((to["plane"] != p) | (to["tile"] != t))
-                def _():
-                    greet(to)
-
-        low = jnp.where((core + y) % 2 == 0, 2, 0)
-        for xx in range(2):
-            greet({"tile": source, "plane": 8 * (low + xx) + zz})
-        return 0
-
-    lax.fori_loop(0, 8, greet_blocks, 0)
-    met = 48 - jnp.where(at_home, 1, 0)
-    for dy, dx in around:
-
-        @pl.when(exists(dy, dx))
+    @pl.when(t == 0)
+    def _():
+        strip_v[...] = jnp.zeros(strip_v.shape, F32)
+
+    for n in range(2 * ITERS):
+
+        @pl.when(xt == 0)
         def _():
-            greet(home_of(c, rr + dy, xt + dx))
-
-        met = met + jnp.where(exists(dy, dx), 1, 0)
-
-    @pl.when(t < TILES - 1)
-    def _():
-        greet(after)
-
-    @pl.when(t > 0)
-    def _():
-        greet(before)
-
-    met = met + jnp.where(t < TILES - 1, 1, 0) + jnp.where(t > 0, 1, 0)
+            hl[n] = jnp.zeros(hl.shape[1:], F32)
+
+        @pl.when(xt == 7)
+        def _():
+            hr[n] = jnp.zeros(hr.shape[1:], F32)
+
+        for at, rows, edge_row in ((0, 0, 0), (1, 10, 2 * TILES - 1)):
+
+            @pl.when(rr == edge_row)
+            def _():
+                yh[n, at] = jnp.zeros(yh.shape[2:], F32)
+                hl[n, rows : rows + 2] = jnp.zeros((2,) + hl.shape[2:], F32)
+                hr[n, rows : rows + 2] = jnp.zeros((2,) + hr.shape[2:], F32)
+
 
     lane = lanes_of((8, 128))
     group = lane // 32
@@ -177,26 +185,30 @@
                     tx[ch * 16 + hh * 8 + half * 4 + q] = tile
 
     def send_blocks(hh):
-        def send(i, _):
-            zz = (pz + far_first(i)) % 8
+        for dz in FAR_FIRST:
+            zz = lax.rem(pz + dz, 8)
             for cc in range(2):
-                xx = 2 * (zz % 4) + cc
-                to = home_of(zz // 4, 2 * t + hh, xx)
-
-                @pl.when((to["plane"] != p) | (to["tile"] != t))
-                def _():
-                    pltpu.make_async_remote_copy(
-                        src_ref=tx.at[(zz // 4) * 16 + hh * 8 + xx],
+                xx = 2 * lax.rem(zz, 4) + cc
+                to = home_of(lax.div(zz, 4), 2 * t + hh, xx)
+
+                def copy():
+                    return pltpu.make_async_remote_copy(
+                        src_ref=tx.at[lax.div(zz, 4) * 16 + hh * 8 + xx],
                         dst_ref=rx.at[pl.ds(pl.multiple_of(p * 8, 8), 8), :],
                         send_sem=in_send,
                         recv_sem=in_recv,
                         device_id=to,
                         device_id_type=MESH,
-                    ).start()
-
-            return 0
-
-        lax.fori_loop(0, 8, send, 0)
+                    )
+
+                if dz == 0:
+
+                    @pl.when((to["plane"] != p) | (to["tile"] != t))
+                    def _():
+                        copy().start()
+
+                else:
+                    copy().start()
 
     for load in loads + strip_loads:
         load.wait()
@@ -385,25 +397,29 @@
     for ys in range(8):
         ot[pl.ds(ys, 32, stride=8), :] = estimate[ys]
 
-    def send_back(i, _):
-        zz = (pz + far_first(i)) % 8
+    for dz in FAR_FIRST:
+        zz = lax.rem(pz + dz, 8)
         for dx in (2, 1, 3, 0):
-            to = 8 * ((px + dx) % 4) + zz
-
-            @pl.when((to != p) | jnp.logical_not(at_home))
-            def _():
-                pltpu.make_async_remote_copy(
+            to = 8 * lax.rem(px + dx, 4) + zz
+
+            def copy():
+                return pltpu.make_async_remote_copy(
                     src_ref=ot.at[pl.ds(pl.multiple_of(to * 8, 8), 8), :],
                     dst_ref=ox.at[slot],
                     send_sem=out_send,
                     recv_sem=out_recv,
                     device_id={"tile": source, "plane": to},
                     device_id_type=MESH,
-                ).start()
-
-        return 0
-
-    lax.fori_loop(0, 8, send_back, 0)
+                )
+
+            if dz + dx == 0:
+
+                @pl.when(jnp.logical_not(at_home))
+                def _():
+                    copy().start()
+
+            else:
+                copy().start()
 
     @pl.when(at_home)
     def _():
@@ -465,7 +481,7 @@
     dma = pltpu.SemaphoreType.DMA
     blocks = pl.pallas_call(
         kernel,
-        out_shape=jax.ShapeDtypeStruct((32, 8, 128), F32),
+        out_shape=pltpu.VMEM((32, 8, 128), F32),
         in_specs=[anywhere, anywhere, scalars, scalars, scalars, scalars],
         out_specs=vmem,
         scratch_shapes=[
@@ -508,7 +524,7 @@
         out_specs=anywhere,
         scratch_shapes=[pltpu.VMEM((256, 128), F32), dma((4,))],
         name="rows_of_blocks",
-    )(blocks)
+    )(pltpu.with_memory_space_constraint(blocks, pltpu.VMEM))
 
 
 def solution(mesh):

time: 46.5 us -> 44.8 us (0.963)
  Pallas kernels: 45 us -> 43.3 us
    pallas_call x1, Pallas kernels: 1.72 us -> 0.82 us  [shards(): pl.pallas_call(to_rows, out_shape=jax.ShapeDtypeStruct(observed.shape, F3...]
    pallas_call x1, Pallas kernels: 43.3 us -> 42.5 us  [shards(): pl.pallas_call(kernel, out_shape=pltpu.VMEM((32, 8, 128), F32), in_specs=...]
where the time goes in v3:
time: 44.8 us; the launch traced here: 44.6 us
  Pallas kernels  43.3 us (97%)
  between operations  1.3 us (3%)
    pallas_call x1, Pallas kernels, shards(): pl.pallas_call(kernel, out_shape=pltpu.VMEM((32, 8, 128), F32), in_specs=...  42.5 us

profile of v3, /device:TPU:1, one launch (start us, length us, event | category | flops | bytes accessed | tf_op | source)
XLA Modules:
  0.0 44.6 jit_solution(4383372483116409105)
XLA Ops:
  1.3 42.5 %richardson_lucy.1.ox = f32[32,8,128]{2,1,0:T(8,128)S(1)} custom-call(f32[2,1,64,256]{3,2,1,0:T(8,128)} %observed.1, f32[2,1,32,256]{3,2,1,0:T(8,128)} %strip.1, f32[2,41]{1,0:T(2,128)} %axial.1, f32[2,15]{1,0:T(2,128)} %lateral.1, s32[1]{0:T(128)S(6)} %copy.7.extents, s32[1]{0:T(128)S(6)} %copy.8.skews), custom_call_target="tpu_custom_call" | custom-call | tf_op jit(solution)/shard_map/richardson_lucy/pallas_call | solution.py:482
  43.8 0.8 %rows_of_blocks.1 = f32[2,1,64,256]{3,2,1,0:T(8,128)} custom-call(f32[32,8,128]{2,1,0:T(8,128)S(1)} %richardson_lucy.1.ox), custom_call_target="tpu_custom_call" | custom-call | tf_op jit(solution)/shard_map/rows_of_blocks/pallas_call | solution.py:520

commit v4 on v3

--- a/solution.py
+++ b/solution.py
@@ -32,21 +32,24 @@
     return value if by == 0 else pltpu.roll(value, by, value.ndim - 1)
 
 
-def build_lateral(taps, out):
+def build_lateral(taps, out, wide):
     lane = lanes_of((32, 128))
     row = lax.broadcasted_iota(jnp.int32, (32, 128), 0)
-    x_out, y_out = lane % 32, lane // 32
-    side, at = row // 8, row % 8
-    own_diff = row - x_out + 7
-    left = at - 8 - x_out + 7
-    right = at + 32 - x_out + 7
-    halo_diff = jnp.where(side == 0, left, jnp.where(side == 3, right, -1))
+    x_lane, y_out = lane % 32, lane // 32
+    x_halo = jnp.where(x_lane < 16, x_lane - 16, x_lane + 16)
+    row_halo = jnp.where(row < 16, row - 16, row + 16)
+    near = (x_lane >= 8) & (x_lane < 24)
+    columns = 2 if wide else 1
     blocks = []
-    for diff in (own_diff, halo_diff):
-        block = jnp.zeros((32, 128), F32)
-        for j in range(KL):
-            block = jnp.where(diff == j, taps[j], block)
-        blocks.append(block)
+    for x_in in (row, row_halo):
+        for o in range(columns):
+            diff = x_in - (x_halo if o else x_lane) + 7
+            if o:
+                diff = jnp.where(near, diff, -1)
+            block = jnp.zeros((32, 128), F32)
+            for j in range(KL):
+                block = jnp.where(diff == j, taps[j], block)
+            blocks.append(block)
     for d in range(5):
         for y_in in range(4):
             line = jnp.zeros((32, 128), F32)
@@ -54,11 +57,12 @@
                 k = 4 * (d - 2) + y_in - y + 7
                 if 0 <= k < KL:
                     line = jnp.where(y_out == y, taps[k], line)
-            for b, block in enumerate(blocks):
-                high, low = split(block * line)
-                rows = pl.ds(b * 640 + d * 128 + y_in * 32, 32)
-                out[rows, 0:128] = high
-                out[rows, 128:256] = low
+            for b in range(2):
+                rows = pl.ds((b * 640 + d * 128 if wide else d * 256 + b * 128) + y_in * 32, 32)
+                for o in range(columns):
+                    high, low = split(blocks[b * columns + o] * line)
+                    out[rows, o * 128 : o * 128 + 128] = high
+                    out[rows, (columns + o) * 128 : (columns + o) * 128 + 128] = low
 
 
 def build_axial(taps, out):
@@ -78,7 +82,7 @@
 
 def kernel(
     observed, strip, axial, lateral, extents, skews, ox,
-    obs_v, strip_s, strip_v, tx, rx, own, sl, sr, hl, hr, yh, eo, eh, wf, wa, zf, za, ot,
+    obs_v, strip_s, strip_v, tx, rx, own, packs, hx, yh, mine, beside, jx, wf, wa, zf, za, ot,
     obs_sem, strip_load, strip_send, strip_recv, in_send, in_recv, halo_send, halo_recv, out_send, out_recv,
 ):
     t = lax.axis_index("tile")
@@ -97,7 +101,7 @@
         fine = (xt + dx >= 0) & (xt + dx < 8)
         return fine & (rr + dy >= 0) & (rr + dy < 2 * TILES)
 
-    around = [(dy, dx) for dy in (-1, 1) for dx in (-1, 1)] + [(0, -1), (0, 1), (-1, 0), (1, 0)]
+    around = [(dy, dx) for dy in (-1, 1) for dx in (-1, 1)] + [(-1, 0), (1, 0), (0, -1), (0, 1)]
     after = {"tile": t + 1, "plane": p}
     before = {"tile": t - 1, "plane": p}
 
@@ -151,24 +155,22 @@
     def _():
         strip_v[...] = jnp.zeros(strip_v.shape, F32)
 
-    for n in range(2 * ITERS):
+    for n in range(ITERS):
 
         @pl.when(xt == 0)
         def _():
-            hl[n] = jnp.zeros(hl.shape[1:], F32)
+            hx[n, 0:2] = jnp.zeros((2,) + hx.shape[2:], F32)
 
         @pl.when(xt == 7)
         def _():
-            hr[n] = jnp.zeros(hr.shape[1:], F32)
-
-        for at, rows, edge_row in ((0, 0, 0), (1, 10, 2 * TILES - 1)):
+            hx[n, 2:4] = jnp.zeros((2,) + hx.shape[2:], F32)
+
+        for at, rows, edge_row in ((0, 0, 0), (1, 12, 2 * TILES - 1)):
 
             @pl.when(rr == edge_row)
             def _():
                 yh[n, at] = jnp.zeros(yh.shape[2:], F32)
-                hl[n, rows : rows + 2] = jnp.zeros((2,) + hl.shape[2:], F32)
-                hr[n, rows : rows + 2] = jnp.zeros((2,) + hr.shape[2:], F32)
-
+                hx[n, :, rows : rows + 4] = jnp.zeros((4, 4) + hx.shape[3:], F32)
 
     lane = lanes_of((8, 128))
     group = lane // 32
@@ -235,13 +237,6 @@
             copy.start()
 
     send_blocks(1)
-
-    lat = [lateral[c, j] for j in range(KL)]
-    ax = [axial[c, j] for j in range(KZ)]
-    build_axial(ax, zf)
-    build_lateral(lat, wf)
-    eo[...] = jnp.zeros(eo.shape, BF16)
-    eh[...] = jnp.zeros(eh.shape, BF16)
 
     @pl.when(t > 0)
     def _():
@@ -274,8 +269,14 @@
     def _():
         rx[pl.ds(pl.multiple_of(p * 8, 8), 8), :] = tx[slot]
 
+    lat = [lateral[c, j] for j in range(KL)]
+    ax = [axial[c, j] for j in range(KZ)]
+    build_axial(ax, zf)
+    build_lateral(lat, wf, True)
+    mine[...] = jnp.zeros(mine.shape, BF16)
+    beside[...] = jnp.zeros(beside.shape, BF16)
     build_axial(ax[::-1], za)
-    build_lateral(lat[::-1], wa)
+    build_lateral(lat[::-1], wa, False)
 
     @pl.when(at_home)
     def _():
@@ -288,50 +289,61 @@
 
     joined = jnp.concatenate([rx[pl.ds(ys, 32, stride=8), :][None] for ys in range(8)], axis=0)
 
-    edge = (lanes_of((8, 8, 128)) // 8) % 4
-    edge2 = (lanes_of((2, 8, 128)) // 8) % 4
     sent = []
 
-    def banded(high, low, w, first, last):
-        both = jnp.dot(high, w[first:last, :], preferred_element_type=F32)
-        more = jnp.dot(low, w[first:last, 0:128], preferred_element_type=F32)
-        return both[:, 0:128] + both[:, 128:256] + more
+    def regroup(lines):
+        group = (lanes_of(lines[0].shape) // 8) % 4
+        done = []
+        for g in range(4):
+            total = turn(lines[0], 8 * (0 - g))
+            for k in range(1, 4):
+                total = jnp.where(group == k, turn(lines[k], 8 * (k - g)), total)
+            done.append(total)
+        return done
+
+    def banded(high, low, w, first):
+        columns, rows = w.shape[1] // 2, pl.ds(first, high.shape[1])
+        both = jnp.dot(high, w[rows, :], preferred_element_type=F32)
+        more = jnp.dot(low, w[rows, 0:columns], preferred_element_type=F32)
+        return both[:, 0:columns] + both[:, columns:] + more
 
     def along_z(flat, z):
-        n = flat.shape[0] // 32
-        high, low = split(flat.reshape(n, 32, 128))
+        n, columns = flat.shape[0] // 32, flat.shape[1]
+        high, low = split(flat.reshape(n, 32, columns))
         stacked = jnp.concatenate([high, low, high], axis=1)
         wide = jnp.concatenate([stacked[i] for i in range(n)], axis=1)
         done = jnp.dot(z[:, 0:96], wide, preferred_element_type=F32)
-        return [done[:, 128 * i : 128 * i + 128] for i in range(n)]
-
-    def shifted(pad, value, w, base):
-        pad[0, 2:10], pad[1, 2:10] = split(value)
-        wide = [jnp.concatenate([pad[s, d : d + 8].reshape(256, 128) for d in range(5)], axis=1) for s in range(2)]
-        return banded(wide[0], wide[1], w, base, base + 640)
-
-    def unpack(left, right, which):
-        sides = [jnp.where(which < 2, turn(left, -8 * k), turn(right, 24 - 8 * k)) for k in range(4)]
-        return jnp.concatenate(sides, axis=1)
-
-    def spread(value, w, z, n):
+        return [done[:, columns * i : columns * (i + 1)] for i in range(n)]
+
+    def padded(pad, value, first):
+        pad[0, 4:12], pad[1, 4:12] = split(value)
+        wide = [jnp.concatenate([pad[i, d : d + 12].reshape(384, 128) for d in range(5)], axis=1) for i in range(2)]
+        return banded(wide[0], wide[1], wf, first)
+
+    def beyond(value, at, first):
+        wide = []
+        for part in split(value):
+            none = jnp.zeros((32, 128), BF16)
+            columns = []
+            for d in range(4):
+                lines = [i + d if at == 0 else i + d - 3 for i in range(4)]
+                columns.append(jnp.concatenate([part[i] if 0 <= i < 4 else none for i in lines], axis=0))
+            wide.append(jnp.concatenate(columns, axis=1))
+        return banded(wide[0], wide[1], wf, first + 128 * at)
+
+    def forward(value, n):
         own[n] = value
-        parts = [value[:, 8 * k : 8 * k + 8, :] for k in range(4)]
-        to_right = turn(parts[0], -24)
-        to_left = parts[0]
-        for k in range(1, 4):
-            to_right = jnp.where(edge == k, turn(parts[k], 8 * k - 24), to_right)
-            to_left = jnp.where(edge == k, turn(parts[k], 8 * k), to_left)
-        sr[n] = to_right
-        sl[n] = to_left
+        for g, pack in enumerate(regroup([value[:, 8 * k : 8 * k + 8, :] for k in range(4)])):
+            packs[n, g] = pack
         copies = {}
         for i, (dy, dx) in enumerate(around):
-            rows, size, at = {-1: (0, 2, 10), 0: (0, 8, 2), 1: (6, 2, 0)}[dy]
+            rows, size, at = {-1: (0, 4, 12), 0: (0, 8, 4), 1: (4, 4, 0)}[dy]
             if dx == 0:
-                src, dst = own.at[n, pl.ds(rows, 2)], yh.at[n, 0 if dy == 1 else 1]
+                src, dst = own.at[n, pl.ds(rows, 4)], yh.at[n, 0 if dy == 1 else 1]
             else:
-                src = (sr if dx == 1 else sl).at[n, pl.ds(rows, size)]
-                dst = (hl if dx == 1 else hr).at[n, pl.ds(at, size)]
+                side = (2, 0) if dx == 1 else (0, 2)
+                src = packs.at[n, pl.ds(side[0], 2), pl.ds(rows, size)]
+                dst = hx.at[n, pl.ds(side[1], 2), pl.ds(at, size)]
             copy = pltpu.make_async_remote_copy(
                 src_ref=src,
                 dst_ref=dst,
@@ -347,52 +359,56 @@
                 copy.start()
 
             sent.append((exists(dy, dx), copy))
-
-        def arrive(dy, dx):
-            @pl.when(exists(-dy, -dx))
-            def _():
-                copies[dy, dx].wait_recv()
-
-        whole = along_z(shifted(eo, value, w, 0), z)
-        arrive(0, 1)
-        arrive(0, -1)
-        beside = unpack(hl[n, 2:10], hr[n, 2:10], edge)
-        sides = along_z(shifted(eh, beside, w, 640), z)
-        whole = [a + b for a, b in zip(whole, sides)]
-        for dy, dx in around:
-            if dy != 0:
-                arrive(dy, dx)
-        ends = []
-        for at, rows in ((0, 0), (1, 10)):
-            corner = unpack(hl[n, rows : rows + 2], hr[n, rows : rows + 2], edge2)
-            ends.append([split(yh[n, at]), split(corner)])
-        flat = []
-        for at in range(2):
-            total = None
-            for b in range(2):
-                wide = []
-                for s in range(2):
-                    pair = ends[at][b][s]
-                    none = jnp.zeros((32, 128), BF16)
-                    if at == 0:
-                        lines = ((pair[0], pair[1]), (pair[1], none))
-                    else:
-                        lines = ((none, pair[0]), (pair[0], pair[1]))
-                    wide.append(jnp.concatenate([jnp.concatenate(line, axis=1) for line in lines], axis=0))
-                first = b * 640 + (0 if at == 0 else 3 * 128)
-                part = banded(wide[0], wide[1], w, first, first + 256)
-                total = part if total is None else total + part
-            flat.append(total)
-        outer = along_z(jnp.concatenate(flat, axis=0), z)
-        for i, ys in enumerate((0, 1, 6, 7)):
-            whole[ys] = whole[ys] + outer[i]
-        return jnp.concatenate([line[None] for line in whole], axis=0)
-
+        def arrive(which):
+            for dy, dx in around:
+                if which(dy):
+
+                    @pl.when(exists(-dy, -dx))
+                    def _():
+                        copies[dy, dx].wait_recv()
+
+        inner = padded(mine, value, 0)
+        arrive(lambda dy: dy == 0)
+        sides = jnp.concatenate(regroup([hx[n, g, 4:12] for g in range(4)]), axis=1)
+        blurred = along_z(inner + padded(beside, sides, 640), zf)
+        arrive(lambda dy: dy != 0)
+        outer = []
+        for at, rows in ((0, 0), (1, 12)):
+            corners = jnp.concatenate(regroup([hx[n, g, rows : rows + 4] for g in range(4)]), axis=1)
+            outer.append(beyond(yh[n, at], at, 0) + beyond(corners, at, 640))
+            if n == 0:
+                edge, near = ((0, 2), (2, 4)) if at == 0 else ((10, 12), (0, 2))
+                jx[edge[0] : edge[1], :, 0:128] = yh[n, at, near[0] : near[1]]
+                jx[edge[0] : edge[1], :, 128:256] = corners[near[0] : near[1]]
+        if n == 0:
+            jx[2:10, :, 0:128] = value
+            jx[2:10, :, 128:256] = sides
+        outer = along_z(jnp.concatenate(outer, axis=0), zf)
+        for i in range(8):
+            o = i if i < 4 else i + 4
+            blurred[o] = blurred[o] + outer[i]
+        return blurred
+
+    def shifts(lines, size):
+        return jnp.concatenate([lines[d : d + size].reshape(size * 32, 256) for d in range(5)], axis=1)
+
+    wide_lane = lanes_of((32, 256))
+    near = (wide_lane // 8) % 4
+    on_slab = (wide_lane < 128) | ((near == 1) & (xt > 0)) | ((near == 2) & (xt < 7))
     estimate = joined
     for sweep in range(ITERS):
-        blurred = spread(estimate, wf, zf, 2 * sweep)
-        quotient = joined / blurred
-        estimate = estimate * spread(quotient, wa, za, 2 * sweep + 1)
+        blurred = forward(estimate, sweep)
+        quotient = []
+        for i in range(12):
+            inside = on_slab
+            if i < 2:
+                inside = inside & (rr > 0)
+            if i >= 10:
+                inside = inside & (rr < 2 * TILES - 1)
+            quotient.append(jnp.where(inside, jx[i] / blurred[i], 0.0)[None])
+        high, low = split(jnp.concatenate(quotient, axis=0))
+        factor = along_z(banded(shifts(high, 8), shifts(low, 8), wa, 0), za)
+        estimate = estimate * jnp.concatenate([line[None] for line in factor], axis=0)
 
     for ys in range(8):
         ot[pl.ds(ys, 32, stride=8), :] = estimate[ys]
@@ -477,7 +493,6 @@
     anywhere = pl.BlockSpec(memory_space=pl.ANY)
     scalars = pl.BlockSpec(memory_space=pltpu.SMEM)
     vmem = pl.BlockSpec(memory_space=pltpu.VMEM)
-    rounds = 2 * ITERS
     dma = pltpu.SemaphoreType.DMA
     blocks = pl.pallas_call(
         kernel,
@@ -490,15 +505,14 @@
             pltpu.VMEM((128, 128), F32),
             pltpu.VMEM((32, 8, 128), F32),
             pltpu.VMEM((256, 128), F32),
-            pltpu.VMEM((rounds, 8, 32, 128), F32),
-            pltpu.VMEM((rounds, 8, 8, 128), F32),
-            pltpu.VMEM((rounds, 8, 8, 128), F32),
-            pltpu.VMEM((rounds, 12, 8, 128), F32),
-            pltpu.VMEM((rounds, 12, 8, 128), F32),
-            pltpu.VMEM((rounds, 2, 2, 32, 128), F32),
-            pltpu.VMEM((2, 12, 32, 128), BF16),
-            pltpu.VMEM((2, 12, 32, 128), BF16),
-            pltpu.VMEM((1280, 256), BF16),
+            pltpu.VMEM((ITERS, 8, 32, 128), F32),
+            pltpu.VMEM((ITERS, 4, 8, 8, 128), F32),
+            pltpu.VMEM((ITERS, 4, 16, 8, 128), F32),
+            pltpu.VMEM((ITERS, 2, 4, 32, 128), F32),
+            pltpu.VMEM((2, 16, 32, 128), BF16),
+            pltpu.VMEM((2, 16, 32, 128), BF16),
+            pltpu.VMEM((12, 32, 256), F32),
+            pltpu.VMEM((1280, 512), BF16),
             pltpu.VMEM((1280, 256), BF16),
             pltpu.VMEM((32, 128), BF16),
             pltpu.VMEM((32, 128), BF16),
@@ -509,8 +523,8 @@
             dma((4,)),
             dma,
             dma,
-            dma((rounds, 8)),
-            dma((rounds, 8)),
+            dma((ITERS, 8)),
+            dma((ITERS, 8)),
             dma,
             dma,
         ],

time: 44.8 us -> 42.2 us (0.942)
  Pallas kernels: 43.3 us -> 40.7 us
    pallas_call x1, Pallas kernels: 42.5 us -> 39.9 us  [shards(): pl.pallas_call(kernel, out_shape=pltpu.VMEM((32, 8, 128), F32), in_specs=...]
where the time goes in v4:
time: 42.2 us; the launch traced here: 42 us
  Pallas kernels  40.7 us (96%)
  between operations  1.3 us (3%)
    pallas_call x1, Pallas kernels, shards(): pl.pallas_call(kernel, out_shape=pltpu.VMEM((32, 8, 128), F32), in_specs=...  39.9 us

profile of v4, /device:TPU:1, one launch (start us, length us, event | category | flops | bytes accessed | tf_op | source)
XLA Modules:
  0.0 42.0 jit_solution(9317779502462443305)
XLA Ops:
  1.3 39.9 %richardson_lucy.1.ox = f32[32,8,128]{2,1,0:T(8,128)S(1)} custom-call(f32[2,1,64,256]{3,2,1,0:T(8,128)} %observed.1, f32[2,1,32,256]{3,2,1,0:T(8,128)} %strip.1, f32[2,41]{1,0:T(2,128)} %axial.1, f32[2,15]{1,0:T(2,128)} %lateral.1, s32[1]{0:T(128)S(6)} %copy.7.extents, s32[1]{0:T(128)S(6)} %copy.8.skews), custom_call_target="tpu_custom_call" | custom-call | tf_op jit(solution)/shard_map/richardson_lucy/pallas_call | solution.py:497
  41.2 0.8 %rows_of_blocks.1 = f32[2,1,64,256]{3,2,1,0:T(8,128)} custom-call(f32[32,8,128]{2,1,0:T(8,128)S(1)} %richardson_lucy.1.ox), custom_call_target="tpu_custom_call" | custom-call | tf_op jit(solution)/shard_map/rows_of_blocks/pallas_call | solution.py:534

commit v5 on v4

--- a/solution.py
+++ b/solution.py
@@ -81,8 +81,9 @@
 
 
 def kernel(
-    observed, strip, axial, lateral, extents, skews, ox,
-    obs_v, strip_s, strip_v, tx, rx, own, packs, hx, yh, mine, beside, jx, wf, wa, zf, za, ot,
+    observed, strip, axial_in, lateral_in, extents_in, skews_in, ox,
+    axial, lateral, extents, skews, small_sem,
+    obs_v, strip_s, strip_v, tx, rx, own, packs, hx, yh, mine, beside, qh, ql, jx, wf, wa, zf, za, ot,
     obs_sem, strip_load, strip_send, strip_recv, in_send, in_recv, halo_send, halo_recv, out_send, out_recv,
 ):
     t = lax.axis_index("tile")
@@ -101,7 +102,7 @@
         fine = (xt + dx >= 0) & (xt + dx < 8)
         return fine & (rr + dy >= 0) & (rr + dy < 2 * TILES)
 
-    around = [(dy, dx) for dy in (-1, 1) for dx in (-1, 1)] + [(-1, 0), (1, 0), (0, -1), (0, 1)]
+    around = [(0, -1), (0, 1)] + [(dy, dx) for dy in (-1, 1) for dx in (-1, 1)] + [(-1, 0), (1, 0)]
     after = {"tile": t + 1, "plane": p}
     before = {"tile": t - 1, "plane": p}
 
@@ -148,7 +149,10 @@
             loads.append(
                 pltpu.make_async_copy(observed.at[ch, 0, :, lanes], obs_v.at[pl.ds(i * 64, 64), :], obs_sem.at[i])
             )
-    for load in strip_loads + loads:
+    scalar_loads = []
+    for i, (src, dst) in enumerate(((axial_in, axial), (lateral_in, lateral), (extents_in, extents), (skews_in, skews))):
+        scalar_loads.append(pltpu.make_async_copy(src, dst, small_sem.at[i]))
+    for load in strip_loads + loads + scalar_loads:
         load.start()
 
     @pl.when(t == 0)
@@ -212,7 +216,7 @@
                 else:
                     copy().start()
 
-    for load in loads + strip_loads:
+    for load in loads + strip_loads + scalar_loads:
         load.wait()
     to_blocks(1)
     pl.semaphore_wait(barrier, met)
@@ -398,16 +402,14 @@
     estimate = joined
     for sweep in range(ITERS):
         blurred = forward(estimate, sweep)
-        quotient = []
         for i in range(12):
             inside = on_slab
             if i < 2:
                 inside = inside & (rr > 0)
             if i >= 10:
                 inside = inside & (rr < 2 * TILES - 1)
-            quotient.append(jnp.where(inside, jx[i] / blurred[i], 0.0)[None])
-        high, low = split(jnp.concatenate(quotient, axis=0))
-        factor = along_z(banded(shifts(high, 8), shifts(low, 8), wa, 0), za)
+            qh[i], ql[i] = split(jnp.where(inside, jx[i] / blurred[i], 0.0))
+        factor = along_z(banded(shifts(qh, 8), shifts(ql, 8), wa, 0), za)
         estimate = estimate * jnp.concatenate([line[None] for line in factor], axis=0)
 
     for ys in range(8):
@@ -491,15 +493,19 @@
 
 def shards(observed, intersection_strip, axial_taps, lateral_taps, extents, section_skews):
     anywhere = pl.BlockSpec(memory_space=pl.ANY)
-    scalars = pl.BlockSpec(memory_space=pltpu.SMEM)
     vmem = pl.BlockSpec(memory_space=pltpu.VMEM)
     dma = pltpu.SemaphoreType.DMA
     blocks = pl.pallas_call(
         kernel,
         out_shape=pltpu.VMEM((32, 8, 128), F32),
-        in_specs=[anywhere, anywhere, scalars, scalars, scalars, scalars],
+        in_specs=[anywhere] * 6,
         out_specs=vmem,
         scratch_shapes=[
+            pltpu.SMEM((2, KZ), F32),
+            pltpu.SMEM((2, KL), F32),
+            pltpu.SMEM((1,), jnp.int32),
+            pltpu.SMEM((1,), jnp.int32),
+            dma((4,)),
             pltpu.VMEM((256, 128), F32),
             pltpu.VMEM((128, 128), F32),
             pltpu.VMEM((128, 128), F32),
@@ -511,6 +517,8 @@
             pltpu.VMEM((ITERS, 2, 4, 32, 128), F32),
             pltpu.VMEM((2, 16, 32, 128), BF16),
             pltpu.VMEM((2, 16, 32, 128), BF16),
+            pltpu.VMEM((12, 32, 256), BF16),
+            pltpu.VMEM((12, 32, 256), BF16),
             pltpu.VMEM((12, 32, 256), F32),
             pltpu.VMEM((1280, 512), BF16),
             pltpu.VMEM((1280, 256), BF16),

time: 42.2 us -> 41.1 us (0.974)
  Pallas kernels: 40.7 us -> 39.7 us
    pallas_call x1, Pallas kernels: 39.9 us -> 38.8 us  [shards(): pl.pallas_call(kernel, out_shape=pltpu.VMEM((32, 8, 128), F32), in_specs=...]
where the time goes in v5:
time: 41.1 us; the launch traced here: 41 us
  Pallas kernels  39.7 us (97%)
  between operations  1.3 us (3%)
    pallas_call x1, Pallas kernels, shards(): pl.pallas_call(kernel, out_shape=pltpu.VMEM((32, 8, 128), F32), in_specs=...  38.8 us

profile of v5, /device:TPU:1, one launch (start us, length us, event | category | flops | bytes accessed | tf_op | source)
XLA Modules:
  0.0 41.0 jit_solution(10390624299527140463)
XLA Ops:
  1.3 38.8 %richardson_lucy.1.ox = f32[32,8,128]{2,1,0:T(8,128)S(1)} custom-call(f32[2,1,64,256]{3,2,1,0:T(8,128)} %observed.1, f32[2,1,32,256]{3,2,1,0:T(8,128)} %strip.1, f32[2,41]{1,0:T(2,128)} %axial_in.1, f32[2,15]{1,0:T(2,128)} %lateral_in.1, s32[1]{0:T(128)S(6)} %copy.7.extents_in, s32[1]{0:T(128)S(6)} %copy.8.skews_in), custom_call_target="tpu_custom_call" | custom-call | tf_op jit(solution)/shard_map/richardson_lucy/pallas_call | solution.py:498
  40.1 0.8 %rows_of_blocks.1 = f32[2,1,64,256]{3,2,1,0:T(8,128)} custom-call(f32[32,8,128]{2,1,0:T(8,128)S(1)} %richardson_lucy.1.ox), custom_call_target="tpu_custom_call" | custom-call | tf_op jit(solution)/shard_map/rows_of_blocks/pallas_call | solution.py:542

commit v6 on v5

--- a/solution.py
+++ b/solution.py
@@ -103,6 +103,8 @@
         return fine & (rr + dy >= 0) & (rr + dy < 2 * TILES)
 
     around = [(0, -1), (0, 1)] + [(dy, dx) for dy in (-1, 1) for dx in (-1, 1)] + [(-1, 0), (1, 0)]
+    homes = {(dy, dx): home_of(c, rr + dy, xt + dx) for dy, dx in around}
+    there = {(dy, dx): exists(dy, dx) for dy, dx in around}
     after = {"tile": t + 1, "plane": p}
     before = {"tile": t - 1, "plane": p}
 
@@ -125,11 +127,11 @@
     met = PLANES - jnp.where(at_home, 1, 0)
     for dy, dx in around:
 
-        @pl.when(exists(dy, dx))
+        @pl.when(there[dy, dx])
         def _():
-            greet(home_of(c, rr + dy, xt + dx))
-
-        met = met + jnp.where(exists(dy, dx), 1, 0)
+            greet(homes[dy, dx])
+
+        met = met + jnp.where(there[dy, dx], 1, 0)
 
     @pl.when(t > 0)
     def _():
@@ -353,33 +355,37 @@
                 dst_ref=dst,
                 send_sem=halo_send.at[n, i],
                 recv_sem=halo_recv.at[n, i],
-                device_id=home_of(c, rr + dy, xt + dx),
+                device_id=homes[dy, dx],
                 device_id_type=MESH,
             )
             copies[dy, dx] = copy
 
-            @pl.when(exists(dy, dx))
+            @pl.when(there[dy, dx])
             def _():
                 copy.start()
 
-            sent.append((exists(dy, dx), copy))
+            sent.append((there[dy, dx], copy))
         def arrive(which):
             for dy, dx in around:
-                if which(dy):
-
-                    @pl.when(exists(-dy, -dx))
+                if which(dy, dx):
+
+                    @pl.when(there[-dy, -dx])
                     def _():
                         copies[dy, dx].wait_recv()
 
-        inner = padded(mine, value, 0)
-        arrive(lambda dy: dy == 0)
+        blurred = along_z(padded(mine, value, 0), zf)
+        arrive(lambda dy, dx: dy == 0)
         sides = jnp.concatenate(regroup([hx[n, g, 4:12] for g in range(4)]), axis=1)
-        blurred = along_z(inner + padded(beside, sides, 640), zf)
-        arrive(lambda dy: dy != 0)
+        side = padded(beside, sides, 640)
+        arrive(lambda dy, dx: dy * dx != 0)
+        corner = [jnp.concatenate(regroup([hx[n, g, r : r + 4] for g in range(4)]), axis=1) for r in (0, 12)]
+        diagonal = [beyond(corner[at], at, 640) for at in range(2)]
+        arrive(lambda dy, dx: dx == 0)
+        straight = [beyond(yh[n, at], at, 0) for at in range(2)]
         outer = []
-        for at, rows in ((0, 0), (1, 12)):
-            corners = jnp.concatenate(regroup([hx[n, g, rows : rows + 4] for g in range(4)]), axis=1)
-            outer.append(beyond(yh[n, at], at, 0) + beyond(corners, at, 640))
+        for at in range(2):
+            corners = corner[at]
+            outer.append(straight[at] + diagonal[at])
             if n == 0:
                 edge, near = ((0, 2), (2, 4)) if at == 0 else ((10, 12), (0, 2))
                 jx[edge[0] : edge[1], :, 0:128] = yh[n, at, near[0] : near[1]]
@@ -387,10 +393,8 @@
         if n == 0:
             jx[2:10, :, 0:128] = value
             jx[2:10, :, 128:256] = sides
-        outer = along_z(jnp.concatenate(outer, axis=0), zf)
-        for i in range(8):
-            o = i if i < 4 else i + 4
-            blurred[o] = blurred[o] + outer[i]
+        rest = jnp.concatenate([side[0:128] + outer[0], side[128:256], side[256:384] + outer[1]], axis=0)
+        blurred = [a + b for a, b in zip(blurred, along_z(rest, zf))]
         return blurred
 
     def shifts(lines, size):
@@ -448,9 +452,9 @@
         for copy in strips:
             copy.wait_send()
 
-    for there, copy in sent:
-
-        @pl.when(there)
+    for used, copy in sent:
+
+        @pl.when(used)
         def _():
             copy.wait_send()
 

time: 41.1 us -> 41 us (level)
  no operation moved by 1% of the time
where the time goes in v6:
time: 41 us; the launch traced here: 40.8 us
  Pallas kernels  39.5 us (96%)
  between operations  1.3 us (3%)
    pallas_call x1, Pallas kernels, shards(): pl.pallas_call(kernel, out_shape=pltpu.VMEM((32, 8, 128), F32), in_specs=...  38.7 us

profile of v6, /device:TPU:1, one launch (start us, length us, event | category | flops | bytes accessed | tf_op | source)
XLA Modules:
  0.0 40.8 jit_solution(9081012328437236675)
XLA Ops:
  1.3 38.7 %richardson_lucy.1.ox = f32[32,8,128]{2,1,0:T(8,128)S(1)} custom-call(f32[2,1,64,256]{3,2,1,0:T(8,128)} %observed.1, f32[2,1,32,256]{3,2,1,0:T(8,128)} %strip.1, f32[2,41]{1,0:T(2,128)} %axial_in.1, f32[2,15]{1,0:T(2,128)} %lateral_in.1, s32[1]{0:T(128)S(6)} %copy.7.extents_in, s32[1]{0:T(128)S(6)} %copy.8.skews_in), custom_call_target="tpu_custom_call" | custom-call | tf_op jit(solution)/shard_map/richardson_lucy/pallas_call | solution.py:502
  40.0 0.8 %rows_of_blocks.1 = f32[2,1,64,256]{3,2,1,0:T(8,128)} custom-call(f32[32,8,128]{2,1,0:T(8,128)S(1)} %richardson_lucy.1.ox), custom_call_target="tpu_custom_call" | custom-call | tf_op jit(solution)/shard_map/rows_of_blocks/pallas_call | solution.py:546
